TPU v7x, 128 devices: a whole 4x4x4 slice. The times are simulated.
128 devices in a mesh: dp: 32 (over z, y, core), graph: 4 (over x).
Axes of the slice: x: 4, y: 4, z: 4, core: 2. Of those that a mesh axis runs over, the one named last changes fastest.
Arguments:
- atoms: bfloat16 [32, 4, 1024, 128], P('dp', 'graph'), may hold values from -80 to 80, as said below
- gain: float32 [128], replicated, may hold values from 0.1 to 1.9
- w_src: bfloat16 [128, 128], replicated, may hold values from -0.5 to 0.5
- w_edge: bfloat16 [128, 128], replicated, may hold values from -0.5 to 0.5
- w_out: bfloat16 [128, 128], replicated, may hold values from -0.5 to 0.5
- send_src: int32 [32, 4, 4, 2048], P('dp', 'graph'), may hold values from 0 to 1023
- recv_dst: int32 [32, 4, 4, 2048], P('dp', 'graph'), may hold values from 0 to 1023
- edge_count: int32 [32, 4, 4], P('dp'), may hold values from 512 to 2048, as said below
- edge_feat: bfloat16 [32, 4, 4, 2048, 128], P('dp', 'graph'), may hold values from -6 to 6
- cotangent: bfloat16 [32, 4, 1024, 128], P('dp', 'graph'), may hold values from -6 to 6
Outputs:
- layer_out: bfloat16 [32, 4, 1024, 128], P('dp', 'graph')
- grad_atoms: bfloat16 [32, 4, 1024, 128], P('dp', 'graph')
- grad_w_src: float32 [128, 128], P('dp')
- grad_w_edge: float32 [128, 128], P('dp')
- grad_w_out: float32 [128, 128], P('dp')
- grad_gain: float32 [128], P('dp')
Inputs may be any that keep to these rules, and one draw needn't show every extreme that they name: `atoms`: row scales of the atom features vary. `edge_count`: every batch has one destination shard that receives more; in every draw some shard sends exactly 2048 live slots to some shard.
All inputs are finite; a program needn't handle non-finite values.
Results may differ from a plain program's by a relative error of at most 0.0059.
Values may be sent and summed in bfloat16 or wider, within the bound.
A program may use at most 64 MiB of HBM per device.

v0:
```python
import jax
import jax.numpy as jnp
from jax import lax
from jax.sharding import PartitionSpec as P

DEG_NORM = 23


def silu_slope(pre):
    sig = jax.nn.sigmoid(pre)
    return sig * (1.0 + pre * (1.0 - sig))


def one_hot_table(index, atom_count):
    return (index[:, None] == jnp.arange(atom_count, dtype=jnp.int32)[None, :]).astype(jnp.bfloat16)


def pick_rows(table, index):
    selector = one_hot_table(index, table.shape[0])
    return jnp.dot(selector, table, preferred_element_type=jnp.float32).astype(table.dtype)


def add_rows(values, index, atom_count):
    selector = one_hot_table(index, atom_count)
    return lax.dot_general(
        selector, values, (((0,), (0,)), ((), ())), preferred_element_type=jnp.float32
    )


def body(atoms, gain, w_src, w_edge, w_out, send_src, recv_dst, edge_count, edge_feat, cotangent):
    shards = lax.axis_size("graph")
    myself = lax.axis_index("graph")
    atom_count = atoms.shape[2]
    chans = atoms.shape[3]
    slots = send_src.shape[3]
    width = w_src.shape[1]
    hfull = atoms.reshape(atom_count, chans).astype(jnp.float32)
    inv = lax.rsqrt(jnp.mean(hfull * hfull, axis=-1) + 1e-06)
    normed = (hfull * inv[:, None] * gain).astype(jnp.bfloat16)
    src_local = send_src.reshape(shards, slots)
    dst_local = recv_dst.reshape(shards, slots)
    counts = edge_count[0]
    send_counts = lax.dynamic_index_in_dim(counts, myself, 0, keepdims=False)
    valid = (
        (jnp.arange(slots, dtype=jnp.int32)[None, :] < send_counts[:, None])
        .astype(jnp.float32)
        .reshape(-1, 1)
    )
    rows = jnp.concatenate([pick_rows(normed, src_local[peer]) for peer in range(shards)], axis=0)
    edge_rows = edge_feat.reshape(-1, edge_feat.shape[4])
    pre = jnp.dot(rows, w_src, preferred_element_type=jnp.float32) + jnp.dot(
        edge_rows, w_edge, preferred_element_type=jnp.float32
    )
    msg = (jax.nn.silu(pre) * valid).astype(jnp.bfloat16).reshape(shards, slots, width)
    arrived = lax.all_to_all(msg, "graph", split_axis=0, concat_axis=0, tiled=True)
    summed = add_rows(arrived[0], dst_local[0], atom_count)
    for peer in range(1, shards):
        summed = summed + add_rows(arrived[peer], dst_local[peer], atom_count)
    agg = (summed / DEG_NORM).astype(jnp.bfloat16)
    layer_out = (hfull + jnp.dot(agg, w_out, preferred_element_type=jnp.float32)).astype(
        jnp.bfloat16
    )
    cot_flat = cotangent.reshape(atom_count, chans)
    back = (
        lax.dot_general(
            cot_flat, w_out, (((1,), (1,)), ((), ())), preferred_element_type=jnp.float32
        )
        / DEG_NORM
    ).astype(jnp.bfloat16)
    outgoing = jnp.stack([pick_rows(back, dst_local[peer]) for peer in range(shards)], axis=0)
    slot_back = lax.all_to_all(outgoing, "graph", split_axis=0, concat_axis=0, tiled=True).reshape(
        -1, width
    )
    dpre = (slot_back.astype(jnp.float32) * silu_slope(pre) * valid).astype(jnp.bfloat16)
    grad_src = lax.dot_general(
        rows, dpre, (((0,), (0,)), ((), ())), preferred_element_type=jnp.float32
    )
    grad_edge = lax.dot_general(
        edge_rows, dpre, (((0,), (0,)), ((), ())), preferred_element_type=jnp.float32
    )
    grad_out = lax.dot_general(
        agg, cot_flat, (((0,), (0,)), ((), ())), preferred_element_type=jnp.float32
    )
    dpre_peers = dpre.reshape(shards, slots, width)
    dpre_atoms = add_rows(dpre_peers[0], src_local[0], atom_count)
    for peer in range(1, shards):
        dpre_atoms = dpre_atoms + add_rows(dpre_peers[peer], src_local[peer], atom_count)
    dnorm = lax.dot_general(
        dpre_atoms,
        w_src.astype(jnp.float32),
        (((1,), (1,)), ((), ())),
        precision=lax.Precision.HIGHEST,
        preferred_element_type=jnp.float32,
    )
    scaled = gain * dnorm
    grad_g = jnp.sum(dnorm * hfull * inv[:, None], axis=0)
    grad_h = (
        cot_flat.astype(jnp.float32)
        + inv[:, None] * scaled
        - hfull * (inv**3)[:, None] * jnp.mean(hfull * scaled, axis=-1, keepdims=True)
    )
    grad_atoms = grad_h.astype(jnp.bfloat16).reshape(atoms.shape)
    totals = lax.psum((grad_src, grad_edge, grad_out, grad_g), "graph")
    final = (
        lax.psum_scatter(totals[0], "dp", scatter_dimension=0, tiled=True),
        lax.psum_scatter(totals[1], "dp", scatter_dimension=0, tiled=True),
        lax.psum_scatter(totals[2], "dp", scatter_dimension=0, tiled=True),
        lax.psum_scatter(totals[3], "dp", scatter_dimension=0, tiled=True),
    )
    return (layer_out.reshape(atoms.shape), grad_atoms, final[0], final[1], final[2], final[3])


def solution(mesh):
    in_specs = (
        P("dp", "graph", None, None),
        P(),
        P(),
        P(),
        P(),
        P("dp", "graph", None, None),
        P("dp", "graph", None, None),
        P("dp", None, None),
        P("dp", "graph", None, None, None),
        P("dp", "graph", None, None),
    )
    out_specs = (
        P("dp", "graph", None, None),
        P("dp", "graph", None, None),
        P("dp", None),
        P("dp", None),
        P("dp", None),
        P("dp"),
    )
    return jax.shard_map(body, mesh=mesh, in_specs=in_specs, out_specs=out_specs, check_vma=False)
```

profile of v0, /device:TPU:0, one launch (start us, length us, event | category | flops | bytes accessed | tf_op | source)
XLA Modules:
  0.0 290.7 jit_solution(8393633028329341268)
XLA Ops:
  7.2 1.0 fusion.82
  8.2 1.2 fusion.55
  9.4 1.7 fusion.42
  11.1 1.7 fusion.43
  12.8 1.7 fusion.44
  14.5 1.7 fusion.45
  16.2 1.6 pad_maximum_fusion.1
  17.8 4.8 %all-to-all-start.1 = ((bf16[4,2048,128]{2,1,0:T(8,128)(2,1)}), bf16[4,2048,128]{2,1,0:T(8,128)(2,1)}, u32[]{:S(2)}, u32[]{:S(2)}) async-start(bf16[4,2048,128]{2,1,0:T(8,128)(2,1)} %pad_maximum_fusion.1), calls=%async_computation.1 | async-start | bytes 4194304 | tf_op jit(solution)/shard_map/all_to_all | solution.py:71
  24.9 1.7 fusion.35
  26.6 1.7 fusion.36
  28.2 1.7 fusion.37
  29.9 1.7 fusion.38
  32.5 2.7 fusion.71
  35.1 14.0 %all-to-all-done.1 = bf16[4,2048,128]{2,1,0:T(8,128)(2,1)} async-done(((bf16[4,2048,128]{2,1,0:T(8,128)(2,1)}), bf16[4,2048,128]{2,1,0:T(8,128)(2,1)}, u32[]{:S(2)}, u32[]{:S(2)}) %all-to-all-start.1) | async-done | bytes 2097184 | tf_op jit(solution)/shard_map/all_to_all | solution.py:71
  49.1 7.1 %fusion.17 = (bf16[8192,128]{1,0:T(8,128)(2,1)S(1)}, bf16[8192,128]{1,0:T(8,128)(2,1)}) fusion(bf16[4,2048,128]{2,1,0:T(8,128)(2,1)} %all-to-all-done.1, f32[8192]{0:T(1024)S(1)} %bitcast.84, f32[8192,128]{1,0:T(8,128)} %fusion.71, bf16[8192,128]{1,0:T(8,128)(2,1)S(1)} %bitcast.81, bf16[128,128]{1,0:T(8,128)(2,1)S(1)} %copy-done.9), kind=kOutput, calls=%fused_computation.27 | convolution fusion | flops 284164096 | bytes 12648448 | tf_op jit(solution)/shard_map/dot_general | solution.py:51
  56.2 2.7 fusion.10
  58.9 3.5 %fusion.6 = f32[1024,128]{1,0:T(8,128)} fusion(s32[2048]{0:T(1024)S(1)} %bitcast.98, bf16[8192,128]{1,0:T(8,128)(2,1)S(1)} %get-tuple-element.27), kind=kOutput, calls=%fused_computation.11 | convolution fusion | flops 538968064 | bytes 1056768 | tf_op jit(solution)/shard_map/dot_general | solution.py:25
  62.4 3.5 %fusion.8 = f32[1024,128]{1,0:T(8,128)} fusion(s32[2048]{0:T(1024)S(1)} %bitcast.96, bf16[8192,128]{1,0:T(8,128)(2,1)S(1)} %get-tuple-element.27), kind=kOutput, calls=%fused_computation.14 | convolution fusion | flops 538968064 | bytes 1056768 | tf_op jit(solution)/shard_map/dot_general | solution.py:25
  65.9 4.4 %all-to-all-start = ((bf16[4,2048,128]{2,1,0:T(8,128)(2,1)}), bf16[4,2048,128]{2,1,0:T(8,128)(2,1)}, u32[]{:S(2)}, u32[]{:S(2)}) async-start(bf16[4,2048,128]{2,1,0:T(8,128)(2,1)} %bitcast.83), calls=%async_computation | async-start | bytes 4194304 | tf_op jit(solution)/shard_map/all_to_all | solution.py:55
  70.4 4.1 %fusion.52 = f32[1024,128]{1,0:T(8,128)S(1)} fusion(f32[1024,128]{1,0:T(8,128)} %fusion.6, f32[1024,128]{1,0:T(8,128)} %fusion.8, f32[1024,128]{1,0:T(8,128)S(1)} %fusion.10, s32[2048]{0:T(1024)S(1)} %bitcast.94, bf16[8192,128]{1,0:T(8,128)(2,1)} %copy-done.3), kind=kOutput, calls=%fused_computation.68 | convolution fusion | flops 539361280 | bytes 2629632 | tf_op jit(solution)/shard_map/dot_general | solution.py:25
  75.0 68.2 %all-reduce.3 = f32[128]{0:T(128)S(1)} all-reduce(f32[128]{0:T(128)S(1)} %get-tuple-element.18), channel_id=5, replica_groups=mesh['dp'=32,'graph'=4] {'dp'}, use_global_device_ids=true, to_apply=%region_10.11.clone | all-reduce | flops 128 | bytes 1024
  143.3 1.2 fusion.72
  144.5 3.1 %convolution_bitcast_fusion = f32[128,128]{0,1:T(8,128)} fusion(bf16[8192,128]{1,0:T(8,128)(2,1)} %copy-done.3, bf16[8192,128]{1,0:T(8,128)(2,1)S(1)} %bitcast.82), kind=kOutput, calls=%fused_computation.78 | convolution fusion | flops 268435456 | bytes 4259840 | tf_op jit(solution)/shard_map/dot_general | solution.py:78
  147.7 1.4 fusion.70
  149.0 3.7 %fusion.3 = f32[1024,128]{1,0:T(8,128)S(1)} fusion(s32[2048]{0:T(1024)S(1)} %bitcast.92, bf16[4,2048,128]{2,1,0:T(8,128)(2,1)} %all-to-all-done), kind=kOutput, calls=%fused_computation.6 | convolution fusion | flops 538968064 | bytes 1056768 | tf_op jit(solution)/shard_map/dot_general | solution.py:25
  152.8 3.7 %fusion.5 = f32[1024,128]{1,0:T(8,128)S(1)} fusion(s32[2048]{0:T(1024)S(1)} %bitcast.90, bf16[4,2048,128]{2,1,0:T(8,128)(2,1)} %all-to-all-done), kind=kOutput, calls=%fused_computation.9 | convolution fusion | flops 538968064 | bytes 1056768 | tf_op jit(solution)/shard_map/dot_general | solution.py:25
  156.5 3.7 %fusion.1 = f32[1024,128]{1,0:T(8,128)S(1)} fusion(s32[2048]{0:T(1024)S(1)} %bitcast.88, bf16[4,2048,128]{2,1,0:T(8,128)(2,1)} %all-to-all-done), kind=kOutput, calls=%fused_computation.3 | convolution fusion | flops 538968064 | bytes 1056768 | tf_op jit(solution)/shard_map/dot_general | solution.py:25
  160.3 3.8 %fusion.53 = bf16[1024,128]{1,0:T(8,128)(2,1)S(1)} fusion(f32[1024,128]{1,0:T(8,128)S(1)} %fusion.1, f32[1024,128]{1,0:T(8,128)S(1)} %fusion.3, f32[1024,128]{1,0:T(8,128)S(1)} %fusion.5, s32[2048]{0:T(1024)S(1)} %bitcast.86, bf16[4,2048,128]{2,1,0:T(8,128)(2,1)} %all-to-all-done), kind=kOutput, calls=%fused_computation.69 | convolution fusion | flops 539623424 | bytes 2367488 | tf_op jit(solution)/shard_map/dot_general | solution.py:25
  165.0 0.9 fusion.56
  165.9 97.0 %all-reduce.8.cloned.1.call-done = (f32[128,128]{1,0:T(8,128)}, f32[128,128]{0,1:T(8,128)}, f32[128,128]{1,0:T(8,128)}) async-done(((f32[128,128]{1,0:T(8,128)}, f32[128,128]{0,1:T(8,128)}, f32[128,128]{1,0:T(8,128)}), (f32[128,128]{1,0:T(8,128)}, f32[128,128]{0,1:T(8,128)}, f32[128,128]{1,0:T(8,128)})) %all-reduce.8.cloned.1.call-update) | async-done | bytes 196624
  262.9 0.9 constant_dynamic-slice_fusion.1
  264.5 18.2 %all-reduce.5 = (f32[4,128]{1,0:T(4,128)}, f32[4,128]{0,1:T(8,128)S(1)}, f32[4,128]{1,0:T(4,128)}, f32[4]{0:T(128)}) all-reduce(f32[4,128]{1,0:T(4,128)S(1)} %get-tuple-element.41, f32[4,128]{0,1:T(8,128)S(1)} %constant_dynamic-slice_fusion.1, f32[4,128]{1,0:T(4,128)S(1)} %get-tuple-element.40, ...), channel_id=1, replica_groups=mesh['dp'=32,'graph'=4] {'graph'}, use_global_device_ids=true, to_apply=%region_2.3 | all-reduce | flops 1540 | bytes 12320 | tf_op jit(solution)/shard_map/psum | solution.py:103
  (54 shorter events, 5.4 us)
Async XLA Ops:
  7.2 42.0 %copy-start = (bf16[1,1,4,2048,128]{4,3,2,1,0:T(8,128)(2,1)S(1)}, bf16[1,1,4,2048,128]{4,3,2,1,0:T(8,128)(2,1)}, u32[]{:S(2)}) copy-start(bf16[1,1,4,2048,128]{4,3,2,1,0:T(8,128)(2,1)} %param.18) | copy-start | bytes 6291460
  17.8 4.8 %copy-start.7 = (s32[1,1,4,2048]{3,2,1,0:T(4,128)S(1)}, s32[1,1,4,2048]{3,2,1,0:T(4,128)}, u32[]{:S(2)}) copy-start(s32[1,1,4,2048]{3,2,1,0:T(4,128)} %param.15) | copy-start | bytes 98308
  17.8 5.6 %copy-start.1 = (bf16[1,1,1024,128]{3,2,1,0:T(8,128)(2,1)S(1)}, bf16[1,1,1024,128]{3,2,1,0:T(8,128)(2,1)}, u32[]{:S(2)}) copy-start(bf16[1,1,1024,128]{3,2,1,0:T(8,128)(2,1)} %param.10) | copy-start | bytes 786436
  17.8 5.9 %copy-start.10 = (u32[128]{0:T(128)S(1)}, u32[128]{0:T(128)}, u32[]{:S(2)}) copy-start(u32[128]{0:T(128)} %constant.36) | copy-start | bytes 1540
  17.8 7.1 %copy-start.8 = (f32[128]{0:T(128)S(1)}, f32[128]{0:T(128)}, u32[]{:S(2)}) copy-start(f32[128]{0:T(128)} %param.11) | copy-start | bytes 1540
  17.8 31.3 %all-to-all-start.1 = ((bf16[4,2048,128]{2,1,0:T(8,128)(2,1)}), bf16[4,2048,128]{2,1,0:T(8,128)(2,1)}, u32[]{:S(2)}, u32[]{:S(2)}) async-start(bf16[4,2048,128]{2,1,0:T(8,128)(2,1)} %pad_maximum_fusion.1), calls=%async_computation.1 | async-start | bytes 4194304 | tf_op jit(solution)/shard_map/all_to_all | solution.py:71
  26.6 5.0 %copy-start.11 = (bf16[2048,128]{1,0:T(8,128)(2,1)}, bf16[2048,128]{1,0:T(8,128)(2,1)S(1)}, u32[]{:S(2)}) copy-start(bf16[2048,128]{1,0:T(8,128)(2,1)S(1)} %fusion.35) | copy-start | bytes 1572868
  28.2 3.4 %copy-start.13 = (bf16[2048,128]{1,0:T(8,128)(2,1)}, bf16[2048,128]{1,0:T(8,128)(2,1)S(1)}, u32[]{:S(2)}) copy-start(bf16[2048,128]{1,0:T(8,128)(2,1)S(1)} %fusion.36) | copy-start | bytes 1572868
  29.9 1.7 copy-start.15
  29.9 2.5 copy-start.6
  31.6 0.8 copy-start.17
  32.5 16.7 %copy-start.9 = (bf16[128,128]{1,0:T(8,128)(2,1)S(1)}, bf16[128,128]{1,0:T(8,128)(2,1)}, u32[]{:S(2)}) copy-start(bf16[128,128]{1,0:T(8,128)(2,1)} %param.13) | copy-start | bytes 98308
  56.2 6.2 %copy-start.3 = (bf16[8192,128]{1,0:T(8,128)(2,1)}, bf16[8192,128]{1,0:T(8,128)(2,1)S(1)}, u32[]{:S(2)}) copy-start(bf16[8192,128]{1,0:T(8,128)(2,1)S(1)} %get-tuple-element.27) | copy-start | bytes 6291460
  65.9 83.1 %all-to-all-start = ((bf16[4,2048,128]{2,1,0:T(8,128)(2,1)}), bf16[4,2048,128]{2,1,0:T(8,128)(2,1)}, u32[]{:S(2)}, u32[]{:S(2)}) async-start(bf16[4,2048,128]{2,1,0:T(8,128)(2,1)} %bitcast.83), calls=%async_computation | async-start | bytes 4194304 | tf_op jit(solution)/shard_map/all_to_all | solution.py:55
  70.3 73.0 %copy-start.2 = (bf16[1,1,1024,128]{3,2,1,0:T(8,128)(2,1)S(1)}, bf16[1,1,1024,128]{3,2,1,0:T(8,128)(2,1)}, u32[]{:S(2)}) copy-start(bf16[1,1,1024,128]{3,2,1,0:T(8,128)(2,1)} %param.19) | copy-start | bytes 786436
  70.4 192.5 %all-reduce.8.cloned.1.call-start = ((), (), s32[]{:S(2)}) async-start(), calls=%async_computation.2 | async-start | bytes 393216
  144.5 3.1 %copy-start.4 = (bf16[8192,128]{1,0:T(8,128)(2,1)S(1)}, bf16[8192,128]{1,0:T(8,128)(2,1)}, u32[]{:S(2)}) copy-start(bf16[8192,128]{1,0:T(8,128)(2,1)} %copy-done.3) | copy-start | bytes 6291460
  144.5 3.1 %copy-start.12 = (bf16[2048,128]{1,0:T(8,128)(2,1)S(1)}, bf16[2048,128]{1,0:T(8,128)(2,1)}, u32[]{:S(2)}) copy-start(bf16[2048,128]{1,0:T(8,128)(2,1)} %copy-done.11) | copy-start | bytes 1572868
  144.5 3.1 %copy-start.14 = (bf16[2048,128]{1,0:T(8,128)(2,1)S(1)}, bf16[2048,128]{1,0:T(8,128)(2,1)}, u32[]{:S(2)}) copy-start(bf16[2048,128]{1,0:T(8,128)(2,1)} %copy-done.13) | copy-start | bytes 1572868
  144.5 3.1 %copy-start.16 = (bf16[2048,128]{1,0:T(8,128)(2,1)S(1)}, bf16[2048,128]{1,0:T(8,128)(2,1)}, u32[]{:S(2)}) copy-start(bf16[2048,128]{1,0:T(8,128)(2,1)} %copy-done.15) | copy-start | bytes 1572868
  144.5 3.2 %copy-start.18 = (bf16[2048,128]{1,0:T(8,128)(2,1)S(1)}, bf16[2048,128]{1,0:T(8,128)(2,1)}, u32[]{:S(2)}) copy-start(bf16[2048,128]{1,0:T(8,128)(2,1)} %copy-done.17) | copy-start | bytes 1572868
  160.3 4.7 %copy-start.5 = (bf16[128,128]{1,0:T(8,128)(2,1)S(1)}, bf16[128,128]{1,0:T(8,128)(2,1)}, u32[]{:S(2)}) copy-start(bf16[128,128]{1,0:T(8,128)(2,1)} %param.14) | copy-start | bytes 98308
Sparse Core Ops, SparseCore 0:
  165.1 97.7 all-reduce.7
where the time goes:
time: 295 us; the launch traced here: 291 us
  waiting for transfers between devices  111 us (38%)
  blocking collectives  86.4 us (29%)
  matrix products  59.9 us (20%)
  between operations  15.5 us (5%)
  starting transfers between devices  9.25 us (3%)
  local copies, waits for them, and re-layouts  5.56 us (2%)
  other arithmetic  3.09 us (1%)
    unnamed x2, waiting for transfers between devices  97 us
    unnamed x1, blocking collectives  68.2 us
    dot_general x8, matrix products, add_rows(): lax.dot_general(selector, values, (((0,), (0,)), ((), ())), preferred_ele...  28.8 us
    psum x1, blocking collectives, body(): totals = lax.psum((grad_src, grad_edge, grad_out, grad_g), 'graph')  18.2 us
    all_to_all x1, waiting for transfers between devices, body(): lax.all_to_all(outgoing, 'graph', split_axis=0, concat_axis=0, tiled=True)  14 us
    dot_general x8, matrix products, pick_rows(): jnp.dot(selector, table, preferred_element_type=jnp.float32)  13.4 us
    dot_general x1, matrix products, body(): jnp.dot(edge_rows, w_edge, preferred_element_type=jnp.float32)  7.05 us
  transfers between devices with their start and end apart: 3, of which 2 were waited for; matrix products, arithmetic and copies ran while one was open for 8% of the time, Pallas kernels for 0%

commit v1 on v0

v1 whole, which is shorter than its diff:
```python
import functools

import jax
import jax.numpy as jnp
from jax import lax
from jax.experimental import pallas as pl
from jax.experimental.pallas import tpu as pltpu
from jax.sharding import PartitionSpec as P

DEG_NORM = 23.0
TILE = 1024
MESH = pl.DeviceIdType.MESH
F32 = jnp.float32
BF16 = jnp.bfloat16
VMEM_LIMIT = 56 << 20


def mm(a, b, ca, cb):
    return lax.dot_general(a, b, (((ca,), (cb,)), ((), ())), preferred_element_type=F32)


def split(x):
    hi = x.astype(BF16)
    return hi, (x - hi.astype(F32)).astype(BF16)


def one_hot(index, atoms):
    rows = lax.broadcasted_iota(jnp.int32, (atoms, index.shape[1]), 0)
    return (rows == index).astype(F32).astype(BF16)


def norm_parts(h):
    return lax.rsqrt(jnp.mean(h * h, axis=-1, keepdims=True) + 1e-06)


def forward_kernel(shards, counts, atoms, gain, w_src, w_edge, src, dst0, dst1, dst2, dst3, feat, own, out1, out2, out3, slope, normed_t):
    me = lax.axis_index("graph")
    atom_count = atoms.shape[0]
    h = atoms[...].astype(F32)
    normed = (h * norm_parts(h) * gain[...]).astype(BF16)
    normed_t[...] = normed.T
    dsts = (dst0, dst1, dst2, dst3)
    outs = (own, out1, out2, out3)
    w_src_t = w_src[...].T
    w_edge_t = w_edge[...].T
    for j in range(shards):
        peer = lax.rem(me + j, shards)
        live = counts[me, peer]

        def contribution(t):
            span = pl.ds(t * TILE, TILE)
            rows_t = mm(normed_t[...], one_hot(src[pl.ds(peer, 1), span], atom_count), 1, 0).astype(BF16)
            pre = mm(w_src_t, rows_t, 1, 0) + mm(w_edge_t, feat[peer, span, :], 1, 1)
            sig = 0.5 * jnp.tanh(0.5 * pre) + 0.5
            slot = t * TILE + lax.broadcasted_iota(jnp.int32, pre.shape, 1)
            sig = jnp.where(slot < live, sig, 0.0)
            msg = (pre * sig).astype(BF16)
            slope[j, :, span] = (sig * (1.0 + pre * (1.0 - sig))).astype(BF16)
            return mm(one_hot(dsts[j][pl.ds(me, 1), span], atom_count), msg, 1, 1)

        first = contribution(0)

        @pl.when(live <= TILE)
        def _():
            outs[j][...] = first.astype(outs[j].dtype)

        @pl.when(live > TILE)
        def _():
            outs[j][...] = (first + contribution(1)).astype(outs[j].dtype)


def backward_kernel(shards, counts, atoms, gain, w_src, w_out, src, dst0, dst1, dst2, dst3, cot0, cot1, cot2, cot3, feat, slope,
                    grad_atoms, grad_src, grad_edge, grad_gain, back, acc, edge_t):
    me = lax.axis_index("graph")
    atom_count = atoms.shape[0]
    dsts = (dst0, dst1, dst2, dst3)
    cots = (cot0, cot1, cot2, cot3)
    for j in range(shards):
        peer = lax.rem(me + j, shards)
        live = counts[me, peer]
        back[...] = (mm(w_out[...], cots[j][...], 1, 1) / DEG_NORM).astype(BF16)

        def contribution(t):
            span = pl.ds(t * TILE, TILE)
            slot_back = mm(back[...], one_hot(dsts[j][pl.ds(me, 1), span], atom_count), 1, 0)
            dpre = (slot_back * slope[j, :, span].astype(F32)).astype(BF16)
            edge = mm(dpre, feat[peer, span, :], 1, 0)
            return edge, mm(one_hot(src[pl.ds(peer, 1), span], atom_count), dpre, 1, 1)

        edge, total = contribution(0)
        if j == 0:
            edge_t[...] = edge
            acc[...] = total
        else:
            edge_t[...] += edge
            acc[...] += total

        @pl.when(live > TILE)
        def _():
            edge, total = contribution(1)
            edge_t[...] += edge
            acc[...] += total

    h = atoms[...].astype(F32)
    inv = norm_parts(h)
    normed = (h * inv * gain[...]).astype(BF16)
    hi, lo = split(acc[...])
    weight = w_src[...]
    dnorm = mm(hi, weight, 1, 1) + mm(lo, weight, 1, 1)
    grad_src[...] = mm(normed, hi, 0, 0) + mm(normed, lo, 0, 0)
    grad_edge[...] = edge_t[...].T
    scaled = gain[...] * dnorm
    grad_gain[...] = jnp.sum(dnorm * h * inv, axis=0, keepdims=True)
    grad_atoms[...] = (
        cots[0][...].astype(F32)
        + inv * scaled
        - h * (inv * inv * inv) * jnp.mean(h * scaled, axis=-1, keepdims=True)
    ).astype(BF16)


def output_kernel(pieces, atoms, cot, w_out, own, in1, in2, in3, grad_src, grad_edge, grad_gain, layer_out, packed, grad_out):
    summed = own[...] + in1[...].astype(F32) + in2[...].astype(F32) + in3[...].astype(F32)
    agg = (summed / DEG_NORM).astype(BF16)
    layer_out[...] = (atoms[...].astype(F32) + mm(agg, w_out[...], 1, 0)).astype(BF16)
    grad_out[...] = mm(agg, cot[...], 0, 0)
    rows = grad_src.shape[0] // pieces
    for i in range(pieces):
        span = pl.ds(i * rows, rows)
        packed[i, 0:rows, :] = grad_src[span, :]
        packed[i, rows:2 * rows, :] = grad_edge[span, :]
        packed[i, 2 * rows:3 * rows, :] = grad_out[span, :]
        packed[i, 3 * rows:4 * rows, :] = jnp.broadcast_to(grad_gain[...], (rows, grad_gain.shape[1]))


def reduce_kernel(pieces, shards, packed, out_src, out_edge, out_out, out_gain, landed, held, send1, recv1, send2, recv2):
    dp = lax.axis_index("dp")
    graph = lax.axis_index("graph")
    barrier = pltpu.get_barrier_semaphore()
    for k in range(1, pieces):
        pl.semaphore_signal(barrier, inc=1, device_id=(lax.rem(dp + k, pieces), graph), device_id_type=MESH)
    for k in range(1, shards):
        pl.semaphore_signal(barrier, inc=1, device_id=(dp, lax.rem(graph + k, shards)), device_id_type=MESH)
    pl.semaphore_wait(barrier, pieces + shards - 2)
    copies = []
    for k in range(1, pieces):
        target = lax.rem(dp + k, pieces)
        copies.append(pltpu.make_async_remote_copy(
            src_ref=packed.at[target], dst_ref=landed.at[k - 1], send_sem=send1.at[k - 1], recv_sem=recv1.at[k - 1],
            device_id=(target, graph), device_id_type=MESH))
        copies[-1].start()
    for copy in copies:
        copy.wait_recv()
    total = packed[dp]
    for k in range(1, pieces):
        total = total + landed[k - 1]
    held[graph] = total
    swaps = []
    for k in range(1, shards):
        swaps.append(pltpu.make_async_remote_copy(
            src_ref=held.at[graph], dst_ref=held.at[graph], send_sem=send2.at[k - 1], recv_sem=recv2.at[k - 1],
            device_id=(dp, lax.rem(graph + k, shards)), device_id_type=MESH))
        swaps[-1].start()
    for copy in copies:
        copy.wait_send()
    for copy in swaps:
        copy.wait()
    total = held[0]
    for k in range(1, shards):
        total = total + held[k]
    rows = out_src.shape[0]
    out_src[...] = total[0:rows, :]
    out_edge[...] = total[rows:2 * rows, :]
    out_out[...] = total[2 * rows:3 * rows, :]
    lanes = total.shape[1]
    gains = jnp.broadcast_to(total[3 * rows:3 * rows + 1, :], (8, lanes))
    out_gain[...] = pltpu.roll(gains, lax.rem(lanes - dp * rows, lanes), 1)[0:1, 0:rows]


def body(dp, shards, atoms, gain, w_src, w_edge, w_out, send_src, recv_dst, edge_count, edge_feat, cotangent):
    atom_count, chans = atoms.shape[2:]
    slots = send_src.shape[3]
    width = w_src.shape[1]
    vmem = pl.BlockSpec(memory_space=pltpu.VMEM)
    smem = pl.BlockSpec(memory_space=pltpu.SMEM)
    shape = jax.ShapeDtypeStruct

    def from_peer(x, j):
        return lax.ppermute(x, "graph", [((i + j) % shards, i) for i in range(shards)])

    def to_peer(x, j):
        return lax.ppermute(x, "graph", [(i, (i + j) % shards) for i in range(shards)])

    params = pltpu.CompilerParams(vmem_limit_bytes=VMEM_LIMIT)
    atoms2 = atoms.reshape(atom_count, chans)
    gain2 = gain.reshape(1, chans)
    src2 = send_src.reshape(shards, slots)
    dst2 = recv_dst.reshape(shards, slots)
    cot2 = cotangent.reshape(atom_count, chans)
    feat = edge_feat.reshape(shards, slots, edge_feat.shape[4])
    counts = edge_count.reshape(shards, shards)
    dsts = [dst2] + [from_peer(dst2, j) for j in range(1, shards)]
    cots = [cot2] + [from_peer(cot2, j) for j in range(1, shards)]
    own, *parts, slope = pl.pallas_call(
        functools.partial(forward_kernel, shards),
        out_shape=[shape((atom_count, width), F32)] + [shape((atom_count, width), BF16)] * (shards - 1)
        + [shape((shards, width, slots), BF16)],
        in_specs=[smem] + [vmem] * (6 + shards),
        out_specs=[vmem] * (shards + 1),
        scratch_shapes=[pltpu.VMEM((chans, atom_count), BF16)],
        compiler_params=params,
        cost_estimate=pl.CostEstimate(flops=12_000_000_000, bytes_accessed=8_000_000, transcendentals=1_000_000),
        name="forward",
    )(counts, atoms2, gain2, w_src, w_edge, src2, *dsts, feat)
    arrived = [to_peer(parts[j - 1], j) for j in range(1, shards)]
    grad_atoms, grad_src, grad_edge, grad_gain = pl.pallas_call(
        functools.partial(backward_kernel, shards),
        out_shape=[shape((atom_count, chans), BF16), shape((chans, width), F32), shape((chans, width), F32), shape((1, chans), F32)],
        in_specs=[smem] + [vmem] * (7 + 2 * shards),
        out_specs=[vmem] * 4,
        scratch_shapes=[pltpu.VMEM((width, atom_count), BF16), pltpu.VMEM((atom_count, width), F32), pltpu.VMEM((width, chans), F32)],
        compiler_params=params,
        cost_estimate=pl.CostEstimate(flops=12_000_000_000, bytes_accessed=8_000_000, transcendentals=0),
        name="backward",
    )(counts, atoms2, gain2, w_src, w_out, src2, *dsts, *cots, feat, slope)
    rows = chans // dp
    layer_out, packed = pl.pallas_call(
        functools.partial(output_kernel, dp),
        out_shape=[shape((atom_count, chans), BF16), shape((dp, 4 * rows, chans), F32)],
        in_specs=[vmem] * 10,
        out_specs=[vmem] * 2,
        scratch_shapes=[pltpu.VMEM((width, chans), F32)],
        compiler_params=params,
        name="output",
    )(atoms2, cot2, w_out, own, *arrived, grad_src, grad_edge, grad_gain)
    piece = (4 * rows, chans)
    out_src, out_edge, out_out, out_gain = pl.pallas_call(
        functools.partial(reduce_kernel, dp, shards),
        out_shape=[shape((rows, width), F32)] * 3 + [shape((1, rows), F32)],
        in_specs=[vmem],
        out_specs=[vmem] * 4,
        scratch_shapes=[
            pltpu.VMEM((dp - 1,) + piece, F32),
            pltpu.VMEM((shards,) + piece, F32),
            pltpu.SemaphoreType.DMA((dp - 1,)),
            pltpu.SemaphoreType.DMA((dp - 1,)),
            pltpu.SemaphoreType.DMA((shards - 1,)),
            pltpu.SemaphoreType.DMA((shards - 1,)),
        ],
        compiler_params=pltpu.CompilerParams(collective_id=0, has_side_effects=True),
        name="reduce",
    )(packed)
    return (layer_out.reshape(atoms.shape), grad_atoms.reshape(atoms.shape), out_src, out_edge, out_out, out_gain.reshape(rows))


def solution(mesh):
    in_specs = (
        P("dp", "graph", None, None),
        P(),
        P(),
        P(),
        P(),
        P("dp", "graph", None, None),
        P("dp", "graph", None, None),
        P("dp", None, None),
        P("dp", "graph", None, None, None),
        P("dp", "graph", None, None),
    )
    out_specs = (
        P("dp", "graph", None, None),
        P("dp", "graph", None, None),
        P("dp", None),
        P("dp", None),
        P("dp", None),
        P("dp"),
    )
    return jax.shard_map(
        functools.partial(body, mesh.shape["dp"], mesh.shape["graph"]),
        mesh=mesh, in_specs=in_specs, out_specs=out_specs, check_vma=False)
```

time: 295 us -> 65.6 us (0.22); the launches traced: 291 us -> 64.9 us
  waiting for transfers between devices: 111 us -> 0.58 us
  blocking collectives: 86.4 us -> 0 us
  matrix products: 59.9 us -> 0 us
  Pallas kernels: 0 us -> 42.5 us
  between operations: 15.5 us -> 0.72 us
  starting transfers between devices: 9.25 us -> 14 us
  other arithmetic: 3.09 us -> 0 us
    unnamed x2 -> x0, waiting for transfers between devices: 97 us -> none
    unnamed x1 -> x0, blocking collectives: 68.2 us -> none
    dot_general x24 -> x0, matrix products: 59.9 us -> none  [the longest x8 28.8 us: add_rows(): lax.dot_general(selector, values, (((0,), (0,)), ((), ())), preferred_ele...]
    pallas_call x0 -> x4, Pallas kernels: none -> 42.5 us  [the longest x1 17.4 us: body(): pl.pallas_call(functools.partial(reduce_kernel, dp, shards), out_shape=[s...]
    psum x1 -> x0, blocking collectives: 18.2 us -> none  [body(): totals = lax.psum((grad_src, grad_edge, grad_out, grad_g), 'graph')]
    all_to_all x2 -> x0, waiting for transfers between devices: 14 us -> none  [the longest x1 14 us: body(): lax.all_to_all(outgoing, 'graph', split_axis=0, concat_axis=0, tiled=True)]
    ppermute x0 -> x9, starting transfers between devices: none -> 14 us  [the longest x6 8.5 us: from_peer(): lax.ppermute(x, 'graph', [((i + j) % shards, i) for i in range(shards)])]
    all_to_all x2 -> x0, starting transfers between devices: 9.21 us -> none  [the longest x1 4.77 us: body(): lax.all_to_all(outgoing, 'graph', split_axis=0, concat_axis=0, tiled=True)]
  transfers between devices with their start and end apart: 3 -> 9, of which waited for: 2 -> 2; matrix products, arithmetic and copies ran while one was open for 8% -> 0% of each run, Pallas kernels for 0% -> 35%
where the time goes in v1:
time: 65.6 us; the launch traced here: 64.9 us
  Pallas kernels  42.5 us (65%)
  starting transfers between devices  14 us (21%)
  local copies, waits for them, and re-layouts  7.1 us (11%)
  between operations  0.72 us (1%)
    pallas_call x1, Pallas kernels, body(): pl.pallas_call(functools.partial(reduce_kernel, dp, shards), out_shape=[s...  17.4 us
    pallas_call x1, Pallas kernels, body(): pl.pallas_call(functools.partial(forward_kernel, shards), out_shape=[shap...  11.3 us
    pallas_call x1, Pallas kernels, body(): pl.pallas_call(functools.partial(backward_kernel, shards), out_shape=[sha...  11.3 us
    ppermute x6, starting transfers between devices, from_peer(): lax.ppermute(x, 'graph', [((i + j) % shards, i) for i in range(shards)])  8.5 us
    unnamed x22, local copies, waits for them, and re-layouts  7.1 us
    ppermute x3, starting transfers between devices, to_peer(): lax.ppermute(x, 'graph', [(i, (i + j) % shards) for i in range(shards)])  5.5 us
    pallas_call x1, Pallas kernels, body(): pl.pallas_call(functools.partial(output_kernel, dp), out_shape=[shape((at...  2.56 us
  transfers between devices with their start and end apart: 9, of which 2 were waited for; matrix products, arithmetic and copies ran while one was open for 0% of the time, Pallas kernels for 35%

profile of v1, /device:TPU:0, one launch (start us, length us, event | category | flops | bytes accessed | tf_op | source)
XLA Modules:
  0.0 64.9 jit_solution(18126560828406157384)
XLA Ops:
  0.6 2.9 %collective-permute-start = (s32[4,2048]{1,0:T(4,128)}, s32[4,2048]{1,0:T(4,128)S(1)}, u32[]{:S(2)}, u32[]{:S(2)}) collective-permute-start(s32[4,2048]{1,0:T(4,128)} %bitcast.23), channel_id=1, source_target_pairs={{1,0},{2,1},{3,2},{0,3},{5,4},{6,5},{7,6},{4,7},{9,8},{10,9},{11,1... | collective-permute-start | bytes 98312 | tf_op jit(solution)/shard_map/ppermute | solution.py:188
  3.6 0.8 %collective-permute-start.1 = (s32[4,2048]{1,0:T(4,128)}, s32[4,2048]{1,0:T(4,128)S(1)}, u32[]{:S(2)}, u32[]{:S(2)}) collective-permute-start(s32[4,2048]{1,0:T(4,128)} %bitcast.24), channel_id=1, source_target_pairs={{2,0},{3,1},{0,2},{1,3},{6,4},{7,5},{4,6},{5,7},{10,8},{11,9},{8,1... | collective-permute-start | bytes 98312 | tf_op jit(solution)/shard_map/ppermute | solution.py:188
  4.4 0.9 %collective-permute-start.2 = (s32[4,2048]{1,0:T(4,128)}, s32[4,2048]{1,0:T(4,128)S(1)}, u32[]{:S(2)}, u32[]{:S(2)}) collective-permute-start(s32[4,2048]{1,0:T(4,128)} %bitcast.25), channel_id=1, source_target_pairs={{3,0},{0,1},{1,2},{2,3},{7,4},{4,5},{5,6},{6,7},{11,8},{8,9},{9,10... | collective-permute-start | bytes 98312 | tf_op jit(solution)/shard_map/ppermute | solution.py:188
  5.3 2.4 %collective-permute-start.6 = (bf16[1024,128]{1,0:T(8,128)(2,1)}, bf16[1024,128]{1,0:T(8,128)(2,1)S(1)}, u32[]{:S(2)}, u32[]{:S(2)}) collective-permute-start(bf16[1024,128]{1,0:T(8,128)(2,1)} %bitcast.13), channel_id=1, source_target_pairs={{1,0},{2,1},{3,2},{0,3},{5,4},{6,5},{7,6},{4,7},{9,8},{10,9},{11,1... | collective-permute-start | bytes 786440 | tf_op jit(solution)/shard_map/ppermute | solution.py:188
  7.6 1.5 %collective-permute-start.7 = (bf16[1024,128]{1,0:T(8,128)(2,1)}, bf16[1024,128]{1,0:T(8,128)(2,1)S(1)}, u32[]{:S(2)}, u32[]{:S(2)}) collective-permute-start(bf16[1024,128]{1,0:T(8,128)(2,1)} %bitcast.14), channel_id=1, source_target_pairs={{2,0},{3,1},{0,2},{1,3},{6,4},{7,5},{4,6},{5,7},{10,8},{11,9},{8,1... | collective-permute-start | bytes 786440 | tf_op jit(solution)/shard_map/ppermute | solution.py:188
  9.1 0.0 collective-permute-start.8
  9.1 0.1 collective-permute-done.1.dst2
  9.2 0.5 collective-permute-done.2.dst3
  9.7 0.0 copy-done.6
  9.7 0.1 copy-done.7
  9.8 0.5 copy-done.8
  10.3 11.3 %forward.1 = (f32[1024,128]{1,0:T(8,128)}, bf16[1024,128]{1,0:T(8,128)(2,1)}, bf16[1024,128]{1,0:T(8,128)(2,1)}, bf16[1024,128]{1,0:T(8,128)(2,1)}, bf16[4,128,2048]{2,1,0:T(8,128)(2,1)}) custom-call(s32[4,4]{1,0:T(4,128)} %bitcast.28, bf16[1024,128]{1,0:T(8,128)(2,1)} %bitcast.10, f32[1,128]{1,0:T(1,128)} %bitcast.30, bf16[128,128]{1,0:T(8,128)(2,1)} %w_src.3, ...), custom_call_target="tpu_custom_call" | custom-call | flops 12000000000 | bytes 8000000 | tf_op jit(solution)/shard_map/forward/pallas_call | solution.py:203
  21.6 2.7 %collective-permute-start.3 = (bf16[1024,128]{1,0:T(8,128)(2,1)}, bf16[1024,128]{1,0:T(8,128)(2,1)S(1)}, u32[]{:S(2)}, u32[]{:S(2)}) collective-permute-start(bf16[1024,128]{1,0:T(8,128)(2,1)} %get-tuple-element.22), channel_id=1, source_target_pairs={{0,1},{1,2},{2,3},{3,0},{4,5},{5,6},{6,7},{7,4},{8,9},{9,10},{10,1... | collective-permute-start | bytes 786440 | tf_op jit(solution)/shard_map/ppermute | solution.py:191
  24.4 1.4 %collective-permute-start.4 = (bf16[1024,128]{1,0:T(8,128)(2,1)}, bf16[1024,128]{1,0:T(8,128)(2,1)S(1)}, u32[]{:S(2)}, u32[]{:S(2)}) collective-permute-start(bf16[1024,128]{1,0:T(8,128)(2,1)} %get-tuple-element.23), channel_id=1, source_target_pairs={{0,2},{1,3},{2,0},{3,1},{4,6},{5,7},{6,4},{7,5},{8,10},{9,11},{10,... | collective-permute-start | bytes 786440 | tf_op jit(solution)/shard_map/ppermute | solution.py:191
  25.7 0.0 collective-permute-done.6.cot1
  25.8 1.4 %collective-permute-start.5 = (bf16[1024,128]{1,0:T(8,128)(2,1)}, bf16[1024,128]{1,0:T(8,128)(2,1)S(1)}, u32[]{:S(2)}, u32[]{:S(2)}) collective-permute-start(bf16[1024,128]{1,0:T(8,128)(2,1)} %get-tuple-element.24), channel_id=1, source_target_pairs={{0,3},{1,0},{2,1},{3,2},{4,7},{5,4},{6,5},{7,6},{8,11},{9,8},{10,9... | collective-permute-start | bytes 786440 | tf_op jit(solution)/shard_map/ppermute | solution.py:191
  27.1 0.0 collective-permute-done.7.cot2
  27.1 0.0 collective-permute-done.8.cot3
  27.2 0.7 %copy-done.4 = bf16[1024,128]{1,0:T(8,128)(2,1)} copy-done((bf16[1024,128]{1,0:T(8,128)(2,1)}, bf16[1024,128]{1,0:T(8,128)(2,1)S(1)}, u32[]{:S(2)}) %copy-start.4) | copy-done | bytes 262168
  27.8 0.1 copy-done.5
  27.9 11.3 %backward.1 = (bf16[1024,128]{1,0:T(8,128)(2,1)}, f32[128,128]{1,0:T(8,128)}, f32[128,128]{1,0:T(8,128)}, f32[1,128]{1,0:T(1,128)}) custom-call(s32[4,4]{1,0:T(4,128)} %bitcast.29, bf16[1024,128]{1,0:T(8,128)(2,1)} %bitcast.11, f32[1,128]{1,0:T(1,128)} %bitcast.31, bf16[128,128]{1,0:T(8,128)(2,1)} %w_src.3, bf16[128,128]{1,0:T(8,128)(2,1)} %w_out.3, ...), custom_call_target="tpu_custom_call" | custom-call | flops 12000000000 | bytes 8000000 | tf_op jit(solution)/shard_map/backward/pallas_call | solution.py:215
  39.2 0.0 collective-permute-done.3.in1
  39.2 0.0 collective-permute-done.4.in2
  39.3 0.6 copy-done
  39.9 0.1 copy-done.1
  40.0 0.1 copy-done.2
  40.1 2.6 %output.1 = (bf16[1024,128]{1,0:T(8,128)(2,1)}, f32[32,16,128]{2,1,0:T(8,128)}) custom-call(bf16[1024,128]{1,0:T(8,128)(2,1)} %bitcast.12, bf16[1024,128]{1,0:T(8,128)(2,1)} %bitcast.17, bf16[128,128]{1,0:T(8,128)(2,1)} %w_out.3, f32[1024,128]{1,0:T(8,128)} %get-tuple-element.21.own, bf16[1024,128]{1,0:T(8,128)(2,1)} %copy-done, ...), custom_call_target="tpu_custom_call" | custom-call | tf_op jit(solution)/shard_map/output/pallas_call | solution.py:226
  42.7 17.4 %reduce.1 = (f32[4,128]{1,0:T(4,128)}, f32[4,128]{1,0:T(4,128)}, f32[4,128]{1,0:T(4,128)}, f32[1,4]{1,0:T(1,128)}) custom-call(f32[32,16,128]{2,1,0:T(8,128)} %get-tuple-element.31.packed), custom_call_target="tpu_custom_call" | custom-call | tf_op jit(solution)/shard_map/reduce/pallas_call | solution.py:236
  60.0 1.2 %copy.20 = f32[4,128]{1,0:T(4,128)} copy(f32[4,128]{1,0:T(4,128)} %get-tuple-element.44) | data formatting | bytes 4096
  61.3 1.3 %copy.21 = f32[4,128]{1,0:T(4,128)} copy(f32[4,128]{1,0:T(4,128)} %get-tuple-element.45) | data formatting | bytes 4096
  62.5 1.2 %copy.22 = f32[4,128]{1,0:T(4,128)} copy(f32[4,128]{1,0:T(4,128)} %get-tuple-element.46) | data formatting | bytes 4096
  63.7 1.2 %copy.23 = f32[4]{0:T(128)} copy(f32[4]{0:T(128)} %bitcast.32) | data formatting | bytes 32
  (12 shorter events, 0.0 us)
Async XLA Ops:
  0.6 8.5 %collective-permute-start = (s32[4,2048]{1,0:T(4,128)}, s32[4,2048]{1,0:T(4,128)S(1)}, u32[]{:S(2)}, u32[]{:S(2)}) collective-permute-start(s32[4,2048]{1,0:T(4,128)} %bitcast.23), channel_id=1, source_target_pairs={{1,0},{2,1},{3,2},{0,3},{5,4},{6,5},{7,6},{4,7},{9,8},{10,9},{11,1... | collective-permute-start | bytes 98312 | tf_op jit(solution)/shard_map/ppermute | solution.py:188
  3.6 5.6 %collective-permute-start.1 = (s32[4,2048]{1,0:T(4,128)}, s32[4,2048]{1,0:T(4,128)S(1)}, u32[]{:S(2)}, u32[]{:S(2)}) collective-permute-start(s32[4,2048]{1,0:T(4,128)} %bitcast.24), channel_id=1, source_target_pairs={{2,0},{3,1},{0,2},{1,3},{6,4},{7,5},{4,6},{5,7},{10,8},{11,9},{8,1... | collective-permute-start | bytes 98312 | tf_op jit(solution)/shard_map/ppermute | solution.py:188
  4.4 5.3 %collective-permute-start.2 = (s32[4,2048]{1,0:T(4,128)}, s32[4,2048]{1,0:T(4,128)S(1)}, u32[]{:S(2)}, u32[]{:S(2)}) collective-permute-start(s32[4,2048]{1,0:T(4,128)} %bitcast.25), channel_id=1, source_target_pairs={{3,0},{0,1},{1,2},{2,3},{7,4},{4,5},{5,6},{6,7},{11,8},{8,9},{9,10... | collective-permute-start | bytes 98312 | tf_op jit(solution)/shard_map/ppermute | solution.py:188
  5.3 20.5 %collective-permute-start.6 = (bf16[1024,128]{1,0:T(8,128)(2,1)}, bf16[1024,128]{1,0:T(8,128)(2,1)S(1)}, u32[]{:S(2)}, u32[]{:S(2)}) collective-permute-start(bf16[1024,128]{1,0:T(8,128)(2,1)} %bitcast.13), channel_id=1, source_target_pairs={{1,0},{2,1},{3,2},{0,3},{5,4},{6,5},{7,6},{4,7},{9,8},{10,9},{11,1... | collective-permute-start | bytes 786440 | tf_op jit(solution)/shard_map/ppermute | solution.py:188
  7.6 19.5 %collective-permute-start.7 = (bf16[1024,128]{1,0:T(8,128)(2,1)}, bf16[1024,128]{1,0:T(8,128)(2,1)S(1)}, u32[]{:S(2)}, u32[]{:S(2)}) collective-permute-start(bf16[1024,128]{1,0:T(8,128)(2,1)} %bitcast.14), channel_id=1, source_target_pairs={{2,0},{3,1},{0,2},{1,3},{6,4},{7,5},{4,6},{5,7},{10,8},{11,9},{8,1... | collective-permute-start | bytes 786440 | tf_op jit(solution)/shard_map/ppermute | solution.py:188
  9.1 0.6 copy-start.6
  9.1 18.0 %collective-permute-start.8 = (bf16[1024,128]{1,0:T(8,128)(2,1)}, bf16[1024,128]{1,0:T(8,128)(2,1)S(1)}, u32[]{:S(2)}, u32[]{:S(2)}) collective-permute-start(bf16[1024,128]{1,0:T(8,128)(2,1)} %bitcast.15), channel_id=1, source_target_pairs={{3,0},{0,1},{1,2},{2,3},{7,4},{4,5},{5,6},{6,7},{11,8},{8,9},{9,10... | collective-permute-start | bytes 786440 | tf_op jit(solution)/shard_map/ppermute | solution.py:188
  9.2 0.6 copy-start.7
  9.7 0.6 copy-start.8
  21.6 17.6 %collective-permute-start.3 = (bf16[1024,128]{1,0:T(8,128)(2,1)}, bf16[1024,128]{1,0:T(8,128)(2,1)S(1)}, u32[]{:S(2)}, u32[]{:S(2)}) collective-permute-start(bf16[1024,128]{1,0:T(8,128)(2,1)} %get-tuple-element.22), channel_id=1, source_target_pairs={{0,1},{1,2},{2,3},{3,0},{4,5},{5,6},{6,7},{7,4},{8,9},{9,10},{10,1... | collective-permute-start | bytes 786440 | tf_op jit(solution)/shard_map/ppermute | solution.py:191
  24.4 14.9 %collective-permute-start.4 = (bf16[1024,128]{1,0:T(8,128)(2,1)}, bf16[1024,128]{1,0:T(8,128)(2,1)S(1)}, u32[]{:S(2)}, u32[]{:S(2)}) collective-permute-start(bf16[1024,128]{1,0:T(8,128)(2,1)} %get-tuple-element.23), channel_id=1, source_target_pairs={{0,2},{1,3},{2,0},{3,1},{4,6},{5,7},{6,4},{7,5},{8,10},{9,11},{10,... | collective-permute-start | bytes 786440 | tf_op jit(solution)/shard_map/ppermute | solution.py:191
  25.8 1.4 %copy-start.3 = (bf16[1024,128]{1,0:T(8,128)(2,1)}, bf16[1024,128]{1,0:T(8,128)(2,1)S(1)}, u32[]{:S(2)}) copy-start(bf16[1024,128]{1,0:T(8,128)(2,1)S(1)} %collective-permute-done.6.cot1) | copy-start | bytes 786436
  25.8 13.5 %collective-permute-start.5 = (bf16[1024,128]{1,0:T(8,128)(2,1)}, bf16[1024,128]{1,0:T(8,128)(2,1)S(1)}, u32[]{:S(2)}, u32[]{:S(2)}) collective-permute-start(bf16[1024,128]{1,0:T(8,128)(2,1)} %get-tuple-element.24), channel_id=1, source_target_pairs={{0,3},{1,0},{2,1},{3,2},{4,7},{5,4},{6,5},{7,6},{8,11},{9,8},{10,9... | collective-permute-start | bytes 786440 | tf_op jit(solution)/shard_map/ppermute | solution.py:191
  27.1 0.7 %copy-start.4 = (bf16[1024,128]{1,0:T(8,128)(2,1)}, bf16[1024,128]{1,0:T(8,128)(2,1)S(1)}, u32[]{:S(2)}) copy-start(bf16[1024,128]{1,0:T(8,128)(2,1)S(1)} %collective-permute-done.7.cot2) | copy-start | bytes 786436
  27.1 0.8 %copy-start.5 = (bf16[1024,128]{1,0:T(8,128)(2,1)}, bf16[1024,128]{1,0:T(8,128)(2,1)S(1)}, u32[]{:S(2)}) copy-start(bf16[1024,128]{1,0:T(8,128)(2,1)S(1)} %collective-permute-done.8.cot3) | copy-start | bytes 786436
  39.2 0.7 %copy-start = (bf16[1024,128]{1,0:T(8,128)(2,1)}, bf16[1024,128]{1,0:T(8,128)(2,1)S(1)}, u32[]{:S(2)}) copy-start(bf16[1024,128]{1,0:T(8,128)(2,1)S(1)} %collective-permute-done.3.in1) | copy-start | bytes 786436
  39.2 0.8 %copy-start.1 = (bf16[1024,128]{1,0:T(8,128)(2,1)}, bf16[1024,128]{1,0:T(8,128)(2,1)S(1)}, u32[]{:S(2)}) copy-start(bf16[1024,128]{1,0:T(8,128)(2,1)S(1)} %collective-permute-done.4.in2) | copy-start | bytes 786436
  39.3 0.8 %copy-start.2 = (bf16[1024,128]{1,0:T(8,128)(2,1)}, bf16[1024,128]{1,0:T(8,128)(2,1)S(1)}, u32[]{:S(2)}) copy-start(bf16[1024,128]{1,0:T(8,128)(2,1)S(1)} %collective-permute-done.5.in3) | copy-start | bytes 786436

commit v2 on v0

v2 whole, which is shorter than its diff:
```python
import functools

import jax
import jax.numpy as jnp
from jax import lax
from jax.experimental import pallas as pl
from jax.experimental.pallas import tpu as pltpu
from jax.sharding import PartitionSpec as P

DEG_NORM = 23.0
TILE = 1024
LANES = 128
MESH = pl.DeviceIdType.MESH
F32 = jnp.float32
BF16 = jnp.bfloat16
I16 = jnp.int16
VMEM_LIMIT = 56 << 20


def mm(a, b, ca, cb):
    return lax.dot_general(a, b, (((ca,), (cb,)), ((), ())), preferred_element_type=F32)


def split(x):
    hi = x.astype(BF16)
    return hi, (x - hi.astype(F32)).astype(BF16)


def ones_where(mask):
    return jnp.where(mask, jnp.array(1, BF16), jnp.array(0, BF16))


def pick_form(index, atoms):
    rows = lax.broadcasted_iota(jnp.int32, (atoms, index.shape[1]), 0).astype(I16)
    return ones_where(rows == index.astype(I16))


def sum_form(index, atoms):
    column = jnp.concatenate([
        jnp.broadcast_to(index[:, k:k + LANES], (LANES, LANES)).astype(F32).T.astype(jnp.int32).astype(I16)
        for k in range(0, index.shape[1], LANES)
    ], 0)
    return jnp.concatenate([
        ones_where((lax.broadcasted_iota(jnp.int32, column.shape, 1) + a).astype(I16) == column)
        for a in range(0, atoms, LANES)
    ], 1)


def layer_kernel(pieces, counts, atoms, gain, w_src, w_edge, w_out, src, dst, cot, feat_hbm,
                 layer_out, grad_atoms, sums,
                 dst_in, cot_in, feat, msg, slope, partial, far_out, far_in, near_out, near_in, acc,
                 pack_a, pack_b, land_a, land_b, held,
                 feat_sem, dst_send, dst_recv, cot_send, cot_recv, part_send, part_recv,
                 a_send, a_recv, b_send, b_recv, s_send, s_recv):
    dp = lax.axis_index("dp")
    me = lax.axis_index("graph")
    shards = 4
    atom_count, chans = atoms.shape
    slots = src.shape[1]
    half_atoms, half_rows = atom_count // 2, acc.shape[0] // 2
    right, left = lax.rem(me + 1, shards), lax.rem(me + shards - 1, shards)

    barrier = pltpu.get_barrier_semaphore()
    for k in range(1, shards):
        pl.semaphore_signal(barrier, inc=1, device_id=(dp, lax.rem(me + k, shards)), device_id_type=MESH)
    for k in range(1, pieces):
        pl.semaphore_signal(barrier, inc=1, device_id=(lax.rem(dp + k, pieces), me), device_id_type=MESH)

    def send(source, target, send_sem, recv_sem, device):
        copy = pltpu.make_async_remote_copy(
            src_ref=source, dst_ref=target, send_sem=send_sem, recv_sem=recv_sem, device_id=device, device_id_type=MESH)
        copy.start()
        return copy

    peers = [lax.rem(me + j, shards) for j in range(shards)]
    loads = [pltpu.make_async_copy(feat_hbm.at[peers[j]], feat.at[j], feat_sem.at[j]) for j in range(shards)]
    for j in (0, 2, 1, 3):
        loads[j].start()

    h = atoms[...].astype(F32)
    inv = lax.rsqrt(jnp.mean(h * h, axis=-1, keepdims=True) + 1e-06)
    normed_t = (h * inv * gain[...]).astype(BF16).T
    w_src_t = w_src[...].T
    w_edge_t = w_edge[...].T
    spans = [pl.ds(t, TILE) for t in range(0, slots, TILE)]

    def forward(j):
        loads[j].wait()
        for t, span in enumerate(spans):
            rows_t = mm(normed_t, pick_form(src[pl.ds(peers[j], 1), span], atom_count), 1, 0).astype(BF16)
            pre = mm(w_src_t, rows_t, 1, 0) + mm(w_edge_t, feat[j, span, :], 1, 1)
            sig = 0.5 * jnp.tanh(0.5 * pre) + 0.5
            slot = t * TILE + lax.broadcasted_iota(jnp.int32, pre.shape, 1)
            sig = jnp.where(slot < counts[me, peers[j]], sig, 0.0)
            msg[j, :, span] = (pre * sig).astype(BF16)
            slope[j, :, span] = sig * (1.0 + pre * (1.0 - sig))

    def targets(j, span):
        return dst[pl.ds(me, 1), span] if j == 0 else dst_in[j - 1, pl.ds(me, 1), span]

    def sum_messages(j):
        total = None
        for span in spans:
            part = mm(msg[j, :, span], sum_form(targets(j, span), atom_count), 1, 0)
            total = part if total is None else total + part
        return total

    def backward(j, cot_j, first):
        back = (mm(w_out[...], cot_j, 1, 1) / DEG_NORM).astype(BF16)
        edge, total = None, None
        for span in spans:
            slot_back = mm(back, pick_form(targets(j, span), atom_count), 1, 0)
            dpre = (slot_back * slope[j, :, span]).astype(BF16)
            e = mm(dpre, feat[j, span, :], 1, 0)
            a = mm(dpre, sum_form(src[pl.ds(peers[j], 1), span], atom_count), 1, 0)
            edge = e if edge is None else edge + e
            total = a if total is None else total + a
        acc[...] = total if first else acc[...] + total
        return edge

    forward(0)
    pl.semaphore_wait(barrier, pieces + shards - 2)
    dst_copies = []
    for k in (2, 1, 3):
        dst_copies.append(send(dst, dst_in.at[shards - k - 1], dst_send.at[shards - k - 1], dst_recv.at[shards - k - 1], (dp, peers[k])))
    cot_left = send(cot, cot_in.at[0], cot_send.at[0], cot_recv.at[0], (dp, left))
    cot_right = send(cot, cot_in.at[2], cot_send.at[1], cot_recv.at[1], (dp, right))
    for j in (2, 1, 3):
        forward(j)
    for copy in dst_copies:
        copy.wait_recv()

    far_out[...] = sum_messages(2).astype(BF16)
    first_half, second_half = pl.ds(0, half_rows), pl.ds(half_rows, half_rows)
    far_right = send(far_out.at[first_half], far_in.at[0], part_send.at[0], part_recv.at[0], (dp, right))
    far_left = send(far_out.at[second_half], far_in.at[1], part_send.at[1], part_recv.at[1], (dp, left))
    partial[0] = sum_messages(0)
    partial[1] = sum_messages(1)
    upper, lower = pl.ds(0, half_atoms), pl.ds(half_atoms, half_atoms)
    cot_left.wait_recv()
    relay_left = send(cot_in.at[0, upper], cot_in.at[1, upper], cot_send.at[2], cot_recv.at[2], (dp, left))
    cot_right.wait_recv()
    relay_right = send(cot_in.at[2, lower], cot_in.at[1, lower], cot_send.at[3], cot_recv.at[3], (dp, right))
    partial[2] = sum_messages(3)
    far_right.wait_recv()
    near_out[0, first_half, :] = (partial[1, first_half, :] + far_in[0].astype(F32)).astype(BF16)
    near_out[0, second_half, :] = partial[1, second_half, :].astype(BF16)
    near_right = send(near_out.at[0], near_in.at[0], part_send.at[2], part_recv.at[2], (dp, right))
    far_left.wait_recv()
    near_out[1, first_half, :] = partial[2, first_half, :].astype(BF16)
    near_out[1, second_half, :] = (partial[2, second_half, :] + far_in[1].astype(F32)).astype(BF16)
    near_left = send(near_out.at[1], near_in.at[1], part_send.at[3], part_recv.at[3], (dp, left))

    edge = backward(0, cot[...], True)
    edge = edge + backward(1, cot_in[0], False)
    edge = edge + backward(3, cot_in[2], False)
    relay_left.wait_recv()
    relay_right.wait_recv()
    edge = edge + backward(2, cot_in[1], False)

    hi, lo = split(acc[...])
    grad_src = mm(normed_t, hi, 1, 1) + mm(normed_t, lo, 1, 1)
    grad_edge = edge.T
    rows = chans // pieces
    for i in range(pieces):
        pack_a[i, 0:rows, :] = grad_src[i * rows:(i + 1) * rows, :]
        pack_a[i, rows:2 * rows, :] = grad_edge[i * rows:(i + 1) * rows, :]
    copies = []
    for k in range(1, pieces):
        target = lax.rem(dp + k, pieces)
        copies.append(send(pack_a.at[target], land_a.at[k - 1], a_send.at[k - 1], a_recv.at[k - 1], (target, me)))

    dnorm = (mm(w_src[...], hi, 1, 0) + mm(w_src[...], lo, 1, 0)).T
    grad_gain = jnp.sum(dnorm * h * inv, axis=0, keepdims=True)
    near_right.wait_recv()
    near_left.wait_recv()
    summed = partial[0] + near_in[0].astype(F32) + near_in[1].astype(F32)
    agg_t = (summed / DEG_NORM).astype(BF16)
    grad_out = mm(agg_t, cot[...], 1, 0)
    gains = jnp.broadcast_to(grad_gain, (rows, chans))
    for i in range(pieces):
        pack_b[i, 0:rows, :] = grad_out[i * rows:(i + 1) * rows, :]
        pack_b[i, rows:2 * rows, :] = gains
    for k in range(1, pieces):
        target = lax.rem(dp + k, pieces)
        copies.append(send(pack_b.at[target], land_b.at[k - 1], b_send.at[k - 1], b_recv.at[k - 1], (target, me)))

    layer_out[...] = (h + mm(agg_t, w_out[...], 0, 0)).astype(BF16)
    scaled = gain[...] * dnorm
    grad_atoms[...] = (
        cot[...].astype(F32) + inv * scaled - h * (inv * inv * inv) * jnp.mean(h * scaled, axis=-1, keepdims=True)
    ).astype(BF16)

    for copy in copies:
        copy.wait_recv()
    total_a, total_b = pack_a[dp], pack_b[dp]
    for k in range(1, pieces):
        total_a = total_a + land_a[k - 1]
        total_b = total_b + land_b[k - 1]
    held[me, 0:2 * rows, :] = total_a
    held[me, 2 * rows:4 * rows, :] = total_b
    swaps = [
        send(held.at[me], held.at[me], s_send.at[k - 1], s_recv.at[k - 1], (dp, peers[k]))
        for k in range(1, shards)
    ]
    for copy in [*copies, *dst_copies, cot_left, cot_right, relay_left, relay_right, far_left, far_right, near_left, near_right]:
        copy.wait_send()
    for copy in swaps:
        copy.wait()
    sums[...] = (held[0] + held[1]) + (held[2] + held[3])


def results_kernel(layer, atoms_grad, sums, layer_out, grad_atoms, out_src, out_edge, out_out, out_gain):
    layer_out[...] = layer[...]
    grad_atoms[...] = atoms_grad[...]
    rows = out_src.shape[0]
    lanes = sums.shape[1]
    out_src[...] = sums[0:rows, :]
    out_edge[...] = sums[rows:2 * rows, :]
    out_out[...] = sums[2 * rows:3 * rows, :]
    gains = jnp.broadcast_to(sums[3 * rows:3 * rows + 1, :], (8, lanes))
    shift = lax.rem(lanes - lax.axis_index("dp") * rows, lanes)
    out_gain[...] = pltpu.roll(gains, shift, 1)[0:1, 0:rows]


def body(dp, shards, atoms, gain, w_src, w_edge, w_out, send_src, recv_dst, edge_count, edge_feat, cotangent):
    atom_count, chans = atoms.shape[2:]
    slots = send_src.shape[3]
    width = w_src.shape[1]
    vmem = pl.BlockSpec(memory_space=pltpu.VMEM)
    smem = pl.BlockSpec(memory_space=pltpu.SMEM)
    shape = jax.ShapeDtypeStruct
    rows = chans // dp
    dma = pltpu.SemaphoreType.DMA
    layer, atoms_grad, sums = pl.pallas_call(
        functools.partial(layer_kernel, dp),
        out_shape=[shape((atom_count, chans), BF16), shape((atom_count, chans), BF16), shape((4 * rows, chans), F32)],
        in_specs=[smem] + [vmem] * 8 + [pl.BlockSpec(memory_space=pl.ANY)],
        out_specs=[vmem] * 3,
        scratch_shapes=[
            pltpu.VMEM((shards - 1, shards, slots), jnp.int32),
            pltpu.VMEM((shards - 1, atom_count, chans), BF16),
            pltpu.VMEM((shards, slots, edge_feat.shape[4]), BF16),
            pltpu.VMEM((shards, width, slots), BF16),
            pltpu.VMEM((shards, width, slots), F32),
            pltpu.VMEM((3, width, atom_count), F32),
            pltpu.VMEM((width, atom_count), BF16),
            pltpu.VMEM((2, width // 2, atom_count), BF16),
            pltpu.VMEM((2, width, atom_count), BF16),
            pltpu.VMEM((2, width, atom_count), BF16),
            pltpu.VMEM((width, atom_count), F32),
            pltpu.VMEM((dp, 2 * rows, chans), F32),
            pltpu.VMEM((dp, 2 * rows, chans), F32),
            pltpu.VMEM((dp - 1, 2 * rows, chans), F32),
            pltpu.VMEM((dp - 1, 2 * rows, chans), F32),
            pltpu.VMEM((shards, 4 * rows, chans), F32),
            dma((shards,)), dma((shards - 1,)), dma((shards - 1,)), dma((4,)), dma((4,)), dma((4,)), dma((4,)),
            dma((dp - 1,)), dma((dp - 1,)), dma((dp - 1,)), dma((dp - 1,)), dma((shards - 1,)), dma((shards - 1,)),
        ],
        compiler_params=pltpu.CompilerParams(collective_id=0, has_side_effects=True, vmem_limit_bytes=VMEM_LIMIT),
        name="layer",
    )(
        edge_count.reshape(shards, shards), atoms.reshape(atom_count, chans), gain.reshape(1, chans), w_src, w_edge, w_out,
        send_src.reshape(shards, slots), recv_dst.reshape(shards, slots), cotangent.reshape(atom_count, chans),
        edge_feat.reshape(shards, slots, edge_feat.shape[4]),
    )
    layer_out, grad_atoms, out_src, out_edge, out_out, out_gain = pl.pallas_call(
        results_kernel,
        out_shape=[shape((atom_count, chans), BF16)] * 2 + [shape((rows, width), F32)] * 3 + [shape((1, rows), F32)],
        in_specs=[vmem] * 3,
        out_specs=[vmem] * 6,
        name="results",
    )(layer, atoms_grad, sums)
    return (layer_out.reshape(atoms.shape), grad_atoms.reshape(atoms.shape), out_src, out_edge, out_out, out_gain.reshape(rows))


def solution(mesh):
    in_specs = (
        P("dp", "graph", None, None),
        P(),
        P(),
        P(),
        P(),
        P("dp", "graph", None, None),
        P("dp", "graph", None, None),
        P("dp", None, None),
        P("dp", "graph", None, None, None),
        P("dp", "graph", None, None),
    )
    out_specs = (
        P("dp", "graph", None, None),
        P("dp", "graph", None, None),
        P("dp", None),
        P("dp", None),
        P("dp", None),
        P("dp"),
    )
    return jax.shard_map(
        functools.partial(body, mesh.shape["dp"], mesh.shape["graph"]),
        mesh=mesh, in_specs=in_specs, out_specs=out_specs, check_vma=False)
```

time: 295 us -> 42.8 us (0.15); the launches traced: 291 us -> 42.6 us
  waiting for transfers between devices: 111 us -> 0 us
  blocking collectives: 86.4 us -> 0 us
  matrix products: 59.9 us -> 0 us
  Pallas kernels: 0 us -> 41.9 us
  between operations: 15.5 us -> 0.64 us
  starting transfers between devices: 9.25 us -> 0 us
  local copies, waits for them, and re-layouts: 5.56 us -> 0 us
  other arithmetic: 3.09 us -> 0 us
    unnamed x2 -> x0, waiting for transfers between devices: 97 us -> none
    unnamed x1 -> x0, blocking collectives: 68.2 us -> none
    dot_general x24 -> x0, matrix products: 59.9 us -> none  [the longest x8 28.8 us: add_rows(): lax.dot_general(selector, values, (((0,), (0,)), ((), ())), preferred_ele...]
    pallas_call x0 -> x2, Pallas kernels: none -> 41.9 us  [the longest x1 40.1 us: body(): pl.pallas_call(functools.partial(layer_kernel, dp), out_shape=[shape((ato...]
    psum x1 -> x0, blocking collectives: 18.2 us -> none  [body(): totals = lax.psum((grad_src, grad_edge, grad_out, grad_g), 'graph')]
    all_to_all x2 -> x0, waiting for transfers between devices: 14 us -> none  [the longest x1 14 us: body(): lax.all_to_all(outgoing, 'graph', split_axis=0, concat_axis=0, tiled=True)]
    all_to_all x2 -> x0, starting transfers between devices: 9.21 us -> none  [the longest x1 4.77 us: body(): lax.all_to_all(outgoing, 'graph', split_axis=0, concat_axis=0, tiled=True)]
    unnamed x44 -> x0, local copies, waits for them, and re-layouts: 3.85 us -> none
  transfers between devices with their start and end apart: 3 -> 0, of which waited for: 2 -> 0; matrix products, arithmetic and copies ran while one was open for 8% -> 0% of each run, Pallas kernels for 0% -> 0%
where the time goes in v2:
time: 42.8 us; the launch traced here: 42.6 us
  Pallas kernels  41.9 us (98%)
  between operations  0.64 us (1%)
    pallas_call x1, Pallas kernels, body(): pl.pallas_call(functools.partial(layer_kernel, dp), out_shape=[shape((ato...  40.1 us
    pallas_call x1, Pallas kernels, body(): pl.pallas_call(results_kernel, out_shape=[shape((atom_count, chans), BF16...  1.85 us

profile of v2, /device:TPU:0, one launch (start us, length us, event | category | flops | bytes accessed | tf_op | source)
XLA Modules:
  0.0 42.6 jit_solution(11990798603430088345)
XLA Ops:
  0.6 40.1 %layer.1 = (bf16[1024,128]{1,0:T(8,128)(2,1)}, bf16[1024,128]{1,0:T(8,128)(2,1)}, f32[16,128]{1,0:T(8,128)}) custom-call(s32[4,4]{1,0:T(4,128)} %bitcast.15, bf16[1024,128]{1,0:T(8,128)(2,1)} %bitcast.11, f32[1,128]{1,0:T(1,128)} %bitcast.16, bf16[128,128]{1,0:T(8,128)(2,1)} %w_src.1, bf16[128,128]{1,0:T(8,128)(2,1)} %w_edge.1, bf16[128,128]{1,0:T(8,128)(2,1)} %w_out.1, ...), custom_call_target="tpu_custom_call" | custom-call | tf_op jit(solution)/shard_map/layer/pallas_call | solution.py:235
  40.7 1.9 %results.1 = (bf16[1024,128]{1,0:T(8,128)(2,1)}, bf16[1024,128]{1,0:T(8,128)(2,1)}, f32[4,128]{1,0:T(4,128)}, f32[4,128]{1,0:T(4,128)}, f32[4,128]{1,0:T(4,128)}, /*index=5*/f32[1,4]{1,0:T(1,128)}) custom-call(bf16[1024,128]{1,0:T(8,128)(2,1)} %get-tuple-element.15.layer, bf16[1024,128]{1,0:T(8,128)(2,1)} %get-tuple-element.16.atoms_grad, ...), custom_call_target="tpu_custom_call" | custom-call | tf_op jit(solution)/shard_map/results/pallas_call | solution.py:267

commit v3 on v2

v3 whole, which is shorter than its diff:
```python
import functools

import jax
import jax.numpy as jnp
from jax import lax
from jax.experimental import pallas as pl
from jax.experimental.pallas import tpu as pltpu
from jax.sharding import PartitionSpec as P

DEG_NORM = 23.0
LANES = 128
MESH = pl.DeviceIdType.MESH
F32 = jnp.float32
BF16 = jnp.bfloat16
I16 = jnp.int16
VMEM_LIMIT = 56 << 20


def mm(a, b, ca, cb):
    return lax.dot_general(a, b, (((ca,), (cb,)), ((), ())), preferred_element_type=F32)


def split(x):
    hi = x.astype(BF16)
    return hi, (x - hi.astype(F32)).astype(BF16)


def ones_where(mask):
    return jnp.where(mask, jnp.array(1, BF16), jnp.array(0, BF16))


def pick_form(index, atoms):
    rows = lax.broadcasted_iota(jnp.int32, (atoms, index.shape[1]), 0).astype(I16)
    return ones_where(rows == index.astype(I16))


def sum_form(index, atoms):
    column = jnp.concatenate([
        jnp.broadcast_to(index[:, k:k + LANES], (LANES, LANES)).astype(F32).T.astype(jnp.int32).astype(I16)
        for k in range(0, index.shape[1], LANES)
    ], 0)
    return jnp.concatenate([
        ones_where((lax.broadcasted_iota(jnp.int32, column.shape, 1) + a).astype(I16) == column)
        for a in range(0, atoms, LANES)
    ], 1)


def layer_kernel(pieces, counts, atoms, gain, w_src, w_edge, w_out, src, dst, cot, feat_hbm,
                 layer_out, grad_atoms, sums,
                 dst_rows, dst_in, cot_in, feat, msg, slope, partial, far_out, far_in, near_out, near_in, acc,
                 pack_a, pack_b, land_a, land_b, held,
                 feat_sem, dst_send, dst_recv, cot_send, cot_recv, part_send, part_recv,
                 a_send, a_recv, b_send, b_recv, s_send, s_recv):
    dp = lax.axis_index("dp")
    me = lax.axis_index("graph")
    shards = 4
    atom_count, chans = atoms.shape
    slots = src.shape[1]
    half_atoms, half_rows = atom_count // 2, acc.shape[0] // 2
    right, left = lax.rem(me + 1, shards), lax.rem(me + shards - 1, shards)

    barrier = pltpu.get_barrier_semaphore()
    for k in range(1, shards):
        pl.semaphore_signal(barrier, inc=1, device_id=(dp, lax.rem(me + k, shards)), device_id_type=MESH)
    for k in range(1, pieces):
        pl.semaphore_signal(barrier, inc=1, device_id=(lax.rem(dp + k, pieces), me), device_id_type=MESH)

    def send(source, target, send_sem, recv_sem, device):
        copy = pltpu.make_async_remote_copy(
            src_ref=source, dst_ref=target, send_sem=send_sem, recv_sem=recv_sem, device_id=device, device_id_type=MESH)
        copy.start()
        return copy

    peers = [lax.rem(me + j, shards) for j in range(shards)]
    loads = [pltpu.make_async_copy(feat_hbm.at[peers[j]], feat.at[j], feat_sem.at[j]) for j in range(shards)]
    for j in (0, 2, 1, 3):
        loads[j].start()

    h = atoms[...].astype(F32)
    inv = lax.rsqrt(jnp.mean(h * h, axis=-1, keepdims=True) + 1e-06)
    normed_t = (h * inv * gain[...]).astype(BF16).T
    w_src_t = w_src[...].T
    w_edge_t = w_edge[...].T
    for k in range(shards):
        dst_rows[k] = dst[k:k + 1, :]

    def forward(j):
        loads[j].wait()
        rows_t = mm(normed_t, pick_form(src[pl.ds(peers[j], 1), :], atom_count), 1, 0).astype(BF16)
        pre = mm(w_src_t, rows_t, 1, 0) + mm(w_edge_t, feat[j], 1, 1)
        sig = 0.5 * jnp.tanh(0.5 * pre) + 0.5
        slot = lax.broadcasted_iota(jnp.int32, pre.shape, 1)
        sig = jnp.where(slot < counts[me, peers[j]], sig, 0.0)
        msg[j] = (pre * sig).astype(BF16)
        slope[j] = sig * (1.0 + pre * (1.0 - sig))

    def targets(j):
        return dst[pl.ds(me, 1), :] if j == 0 else dst_in[j - 1]

    def sum_messages(j):
        return mm(msg[j], sum_form(targets(j), atom_count), 1, 0)

    def backward(j, cot_j):
        back = (mm(w_out[...], cot_j, 1, 1) / DEG_NORM).astype(BF16)
        slot_back = mm(back, pick_form(targets(j), atom_count), 1, 0)
        dpre = (slot_back * slope[j]).astype(BF16)
        total = mm(dpre, sum_form(src[pl.ds(peers[j], 1), :], atom_count), 1, 0)
        acc[...] = total if j == 0 else acc[...] + total
        return mm(dpre, feat[j], 1, 0)

    forward(0)
    pl.semaphore_wait(barrier, pieces + shards - 2)
    dst_copies = []
    for k in (2, 1, 3):
        slot = shards - k - 1
        dst_copies.append(send(dst_rows.at[peers[k]], dst_in.at[slot], dst_send.at[slot], dst_recv.at[slot], (dp, peers[k])))
    upper, lower = pl.ds(0, half_atoms), pl.ds(half_atoms, half_atoms)
    cot_left = [
        send(cot.at[part], cot_in.at[0, part], cot_send.at[n], cot_recv.at[n], (dp, left)) for n, part in ((0, upper), (1, lower))
    ]
    cot_right = [
        send(cot.at[part], cot_in.at[2, part], cot_send.at[n], cot_recv.at[n], (dp, right)) for n, part in ((2, lower), (3, upper))
    ]
    for j in (2, 1, 3):
        forward(j)
    for copy in dst_copies:
        copy.wait_recv()

    far_out[...] = sum_messages(2).astype(BF16)
    first_half, second_half = pl.ds(0, half_rows), pl.ds(half_rows, half_rows)
    far_right = send(far_out.at[first_half], far_in.at[0], part_send.at[0], part_recv.at[0], (dp, right))
    far_left = send(far_out.at[second_half], far_in.at[1], part_send.at[1], part_recv.at[1], (dp, left))
    partial[1] = sum_messages(1)
    partial[2] = sum_messages(3)
    partial[0] = sum_messages(0)
    edge = backward(0, cot[...])
    cot_left[0].wait_recv()
    relay_left = send(cot_in.at[0, upper], cot_in.at[1, upper], cot_send.at[4], cot_recv.at[4], (dp, left))
    cot_right[0].wait_recv()
    relay_right = send(cot_in.at[2, lower], cot_in.at[1, lower], cot_send.at[5], cot_recv.at[5], (dp, right))
    far_right.wait_recv()
    near_out[0, first_half, :] = (partial[1, first_half, :] + far_in[0].astype(F32)).astype(BF16)
    near_out[0, second_half, :] = partial[1, second_half, :].astype(BF16)
    near_right = send(near_out.at[0], near_in.at[0], part_send.at[2], part_recv.at[2], (dp, right))
    far_left.wait_recv()
    near_out[1, first_half, :] = partial[2, first_half, :].astype(BF16)
    near_out[1, second_half, :] = (partial[2, second_half, :] + far_in[1].astype(F32)).astype(BF16)
    near_left = send(near_out.at[1], near_in.at[1], part_send.at[3], part_recv.at[3], (dp, left))

    cot_left[1].wait_recv()
    edge = edge + backward(1, cot_in[0])
    cot_right[1].wait_recv()
    edge = edge + backward(3, cot_in[2])
    relay_left.wait_recv()
    relay_right.wait_recv()
    grad_out = (
        mm(partial[0].astype(BF16), cot[...], 1, 0) + mm(partial[1].astype(BF16), cot_in[0], 1, 0)
        + mm(far_out[...], cot_in[1], 1, 0) + mm(partial[2].astype(BF16), cot_in[2], 1, 0)
    ) / DEG_NORM
    rows = chans // pieces
    copies = []
    for i in range(pieces):
        pack_b[i] = grad_out[i * rows:(i + 1) * rows, :]
    for k in range(1, pieces):
        target = lax.rem(dp + k, pieces)
        copies.append(send(pack_b.at[target], land_b.at[k - 1], b_send.at[k - 1], b_recv.at[k - 1], (target, me)))
    edge = edge + backward(2, cot_in[1])

    hi, lo = split(acc[...])
    grad_src = mm(normed_t, hi, 1, 1) + mm(normed_t, lo, 1, 1)
    grad_edge = edge.T
    for i in range(pieces):
        pack_a[i, 0:rows, :] = grad_src[i * rows:(i + 1) * rows, :]
        pack_a[i, rows:2 * rows, :] = grad_edge[i * rows:(i + 1) * rows, :]
    for k in range(1, pieces):
        target = lax.rem(dp + k, pieces)
        copies.append(send(pack_a.at[target], land_a.at[k - 1], a_send.at[k - 1], a_recv.at[k - 1], (target, me)))

    dnorm = (mm(w_src[...], hi, 1, 0) + mm(w_src[...], lo, 1, 0)).T
    scaled = gain[...] * dnorm
    grad_atoms[...] = (
        cot[...].astype(F32) + inv * scaled - h * (inv * inv * inv) * jnp.mean(h * scaled, axis=-1, keepdims=True)
    ).astype(BF16)
    near_right.wait_recv()
    near_left.wait_recv()
    summed = partial[0] + near_in[0].astype(F32) + near_in[1].astype(F32)
    layer_out[...] = (h + mm((summed / DEG_NORM).astype(BF16), w_out[...], 0, 0)).astype(BF16)

    for copy in copies:
        copy.wait_recv()
    total_a, total_b = pack_a[dp], pack_b[dp]
    for k in range(1, pieces):
        total_a = total_a + land_a[k - 1]
        total_b = total_b + land_b[k - 1]
    held[me, 0:2 * rows, :] = total_a
    held[me, 2 * rows:3 * rows, :] = total_b
    swaps = [
        send(held.at[me], held.at[me], s_send.at[k - 1], s_recv.at[k - 1], (dp, peers[k]))
        for k in range(1, shards)
    ]
    for copy in [*copies, *dst_copies, *cot_left, *cot_right, relay_left, relay_right, far_left, far_right, near_left, near_right]:
        copy.wait_send()
    for copy in swaps:
        copy.wait()
    sums[...] = (held[0] + held[1]) + (held[2] + held[3])


def results_kernel(gain, w_src, layer, atoms_grad, sums, layer_out, grad_atoms, out_src, out_edge, out_out, out_gain):
    layer_out[...] = layer[...]
    grad_atoms[...] = atoms_grad[...]
    rows, lanes = out_src.shape
    first = lax.axis_index("dp") * rows
    grad_src = sums[0:rows, :]
    out_src[...] = grad_src
    out_edge[...] = sums[rows:2 * rows, :]
    out_out[...] = sums[2 * rows:3 * rows, :]
    row = lax.broadcasted_iota(jnp.int32, (rows, lanes), 0)
    lane = lax.broadcasted_iota(jnp.int32, (rows, lanes), 1)
    mine = mm(ones_where(lane == row + first), w_src[...], 1, 0)
    weighted = jnp.sum(mine * grad_src, axis=1, keepdims=True)
    spread = jnp.sum(jnp.where(lane == row, weighted, 0.0), axis=0, keepdims=True)
    gains = pltpu.roll(jnp.broadcast_to(gain[...], (8, lanes)), lax.rem(lanes - first, lanes), 1)
    out_gain[...] = spread[:, 0:rows] / gains[0:1, 0:rows]


def body(dp, shards, atoms, gain, w_src, w_edge, w_out, send_src, recv_dst, edge_count, edge_feat, cotangent):
    atom_count, chans = atoms.shape[2:]
    slots = send_src.shape[3]
    width = w_src.shape[1]
    vmem = pl.BlockSpec(memory_space=pltpu.VMEM)
    smem = pl.BlockSpec(memory_space=pltpu.SMEM)
    shape = jax.ShapeDtypeStruct
    rows = chans // dp
    dma = pltpu.SemaphoreType.DMA
    layer, atoms_grad, sums = pl.pallas_call(
        functools.partial(layer_kernel, dp),
        out_shape=[shape((atom_count, chans), BF16), shape((atom_count, chans), BF16), shape((3 * rows, chans), F32)],
        in_specs=[smem] + [vmem] * 8 + [pl.BlockSpec(memory_space=pl.ANY)],
        out_specs=[vmem] * 3,
        scratch_shapes=[
            pltpu.VMEM((shards, 1, slots), jnp.int32),
            pltpu.VMEM((shards - 1, 1, slots), jnp.int32),
            pltpu.VMEM((shards - 1, atom_count, chans), BF16),
            pltpu.VMEM((shards, slots, edge_feat.shape[4]), BF16),
            pltpu.VMEM((shards, width, slots), BF16),
            pltpu.VMEM((shards, width, slots), F32),
            pltpu.VMEM((3, width, atom_count), F32),
            pltpu.VMEM((width, atom_count), BF16),
            pltpu.VMEM((2, width // 2, atom_count), BF16),
            pltpu.VMEM((2, width, atom_count), BF16),
            pltpu.VMEM((2, width, atom_count), BF16),
            pltpu.VMEM((width, atom_count), F32),
            pltpu.VMEM((dp, 2 * rows, chans), F32),
            pltpu.VMEM((dp, rows, chans), F32),
            pltpu.VMEM((dp - 1, 2 * rows, chans), F32),
            pltpu.VMEM((dp - 1, rows, chans), F32),
            pltpu.VMEM((shards, 3 * rows, chans), F32),
            dma((shards,)), dma((shards - 1,)), dma((shards - 1,)), dma((6,)), dma((6,)), dma((4,)), dma((4,)),
            dma((dp - 1,)), dma((dp - 1,)), dma((dp - 1,)), dma((dp - 1,)), dma((shards - 1,)), dma((shards - 1,)),
        ],
        compiler_params=pltpu.CompilerParams(collective_id=0, has_side_effects=True, vmem_limit_bytes=VMEM_LIMIT),
        name="layer",
    )(
        edge_count.reshape(shards, shards), atoms.reshape(atom_count, chans), gain.reshape(1, chans), w_src, w_edge, w_out,
        send_src.reshape(shards, slots), recv_dst.reshape(shards, slots), cotangent.reshape(atom_count, chans),
        edge_feat.reshape(shards, slots, edge_feat.shape[4]),
    )
    layer_out, grad_atoms, out_src, out_edge, out_out, out_gain = pl.pallas_call(
        results_kernel,
        out_shape=[shape((atom_count, chans), BF16)] * 2 + [shape((rows, width), F32)] * 3 + [shape((1, rows), F32)],
        in_specs=[vmem] * 5,
        out_specs=[vmem] * 6,
        name="results",
    )(gain.reshape(1, chans), w_src, layer, atoms_grad, sums)
    return (layer_out.reshape(atoms.shape), grad_atoms.reshape(atoms.shape), out_src, out_edge, out_out, out_gain.reshape(rows))


def solution(mesh):
    in_specs = (
        P("dp", "graph", None, None),
        P(),
        P(),
        P(),
        P(),
        P("dp", "graph", None, None),
        P("dp", "graph", None, None),
        P("dp", None, None),
        P("dp", "graph", None, None, None),
        P("dp", "graph", None, None),
    )
    out_specs = (
        P("dp", "graph", None, None),
        P("dp", "graph", None, None),
        P("dp", None),
        P("dp", None),
        P("dp", None),
        P("dp"),
    )
    return jax.shard_map(
        functools.partial(body, mesh.shape["dp"], mesh.shape["graph"]),
        mesh=mesh, in_specs=in_specs, out_specs=out_specs, check_vma=False)
```

time: 42.8 us -> 39.8 us (0.930)
  Pallas kernels: 41.9 us -> 38.9 us
    pallas_call x1, Pallas kernels: 40.1 us -> 36.9 us  [body(): pl.pallas_call(functools.partial(layer_kernel, dp), out_shape=[shape((ato...]
where the time goes in v3:
time: 39.8 us; the launch traced here: 39.5 us
  Pallas kernels  38.9 us (98%)
  between operations  0.64 us (2%)
    pallas_call x1, Pallas kernels, body(): pl.pallas_call(functools.partial(layer_kernel, dp), out_shape=[shape((ato...  36.9 us
    pallas_call x1, Pallas kernels, body(): pl.pallas_call(results_kernel, out_shape=[shape((atom_count, chans), BF16...  2.01 us

profile of v3, /device:TPU:0, one launch (start us, length us, event | category | flops | bytes accessed | tf_op | source)
XLA Modules:
  0.0 39.5 jit_solution(15642072020795375432)
XLA Ops:
  0.6 36.9 %layer.1 = (bf16[1024,128]{1,0:T(8,128)(2,1)}, bf16[1024,128]{1,0:T(8,128)(2,1)}, f32[12,128]{1,0:T(8,128)}) custom-call(s32[4,4]{1,0:T(4,128)} %bitcast.15, bf16[1024,128]{1,0:T(8,128)(2,1)} %bitcast.11, f32[1,128]{1,0:T(1,128)} %bitcast.16, bf16[128,128]{1,0:T(8,128)(2,1)} %w_src.3, bf16[128,128]{1,0:T(8,128)(2,1)} %w_edge.1, bf16[128,128]{1,0:T(8,128)(2,1)} %w_out.1, ...), custom_call_target="tpu_custom_call" | custom-call | tf_op jit(solution)/shard_map/layer/pallas_call | solution.py:235
  37.5 2.0 %results.1 = (bf16[1024,128]{1,0:T(8,128)(2,1)}, bf16[1024,128]{1,0:T(8,128)(2,1)}, f32[4,128]{1,0:T(4,128)}, f32[4,128]{1,0:T(4,128)}, f32[4,128]{1,0:T(4,128)}, /*index=5*/f32[1,4]{1,0:T(1,128)}) custom-call(f32[1,128]{1,0:T(1,128)} %bitcast.17, bf16[128,128]{1,0:T(8,128)(2,1)} %w_src.3, bf16[1024,128]{1,0:T(8,128)(2,1)} %get-tuple-element.15.layer, ...), custom_call_target="tpu_custom_call" | custom-call | tf_op jit(solution)/shard_map/results/pallas_call | solution.py:268

commit v4 on v3

--- a/solution.py
+++ b/solution.py
@@ -50,7 +50,7 @@
                  dst_rows, dst_in, cot_in, feat, msg, slope, partial, far_out, far_in, near_out, near_in, acc,
                  pack_a, pack_b, land_a, land_b, held,
                  feat_sem, dst_send, dst_recv, cot_send, cot_recv, part_send, part_recv,
-                 a_send, a_recv, b_send, b_recv, s_send, s_recv):
+                 a_send, a_recv, b_send, b_recv, s_send, s_recv, ready_y, ready_core):
     dp = lax.axis_index("dp")
     me = lax.axis_index("graph")
     shards = 4
@@ -62,8 +62,14 @@
     barrier = pltpu.get_barrier_semaphore()
     for k in range(1, shards):
         pl.semaphore_signal(barrier, inc=1, device_id=(dp, lax.rem(me + k, shards)), device_id_type=MESH)
-    for k in range(1, pieces):
-        pl.semaphore_signal(barrier, inc=1, device_id=(lax.rem(dp + k, pieces), me), device_id_type=MESH)
+    ring = pieces // 2
+    side = 4
+    core, row, plane = lax.rem(dp, 2), lax.rem(dp // 2, side), dp // (2 * side)
+    other = dp + 1 - 2 * core
+    along_y = [dp + 2 * (lax.rem(row + k, side) - row) for k in range(1, side)]
+    along_z = [dp + 2 * side * (lax.rem(plane + k, ring // side) - plane) for k in range(1, ring // side)]
+    for peer in (other, *along_y, *along_z):
+        pl.semaphore_signal(barrier, inc=1, device_id=(peer, me), device_id_type=MESH)
 
     def send(source, target, send_sem, recv_sem, device):
         copy = pltpu.make_async_remote_copy(
@@ -73,7 +79,7 @@
 
     peers = [lax.rem(me + j, shards) for j in range(shards)]
     loads = [pltpu.make_async_copy(feat_hbm.at[peers[j]], feat.at[j], feat_sem.at[j]) for j in range(shards)]
-    for j in (0, 2, 1, 3):
+    for j in (2, 1, 3, 0):
         loads[j].start()
 
     h = atoms[...].astype(F32)
@@ -108,36 +114,36 @@
         acc[...] = total if j == 0 else acc[...] + total
         return mm(dpre, feat[j], 1, 0)
 
-    forward(0)
-    pl.semaphore_wait(barrier, pieces + shards - 2)
+    forward(2)
+    pl.semaphore_wait(barrier, shards + len(along_y) + len(along_z))
     dst_copies = []
     for k in (2, 1, 3):
         slot = shards - k - 1
         dst_copies.append(send(dst_rows.at[peers[k]], dst_in.at[slot], dst_send.at[slot], dst_recv.at[slot], (dp, peers[k])))
     upper, lower = pl.ds(0, half_atoms), pl.ds(half_atoms, half_atoms)
-    cot_left = [
-        send(cot.at[part], cot_in.at[0, part], cot_send.at[n], cot_recv.at[n], (dp, left)) for n, part in ((0, upper), (1, lower))
-    ]
-    cot_right = [
-        send(cot.at[part], cot_in.at[2, part], cot_send.at[n], cot_recv.at[n], (dp, right)) for n, part in ((2, lower), (3, upper))
-    ]
-    for j in (2, 1, 3):
-        forward(j)
+    cot_left = [send(cot.at[upper], cot_in.at[0, upper], cot_send.at[0], cot_recv.at[0], (dp, left))]
+    cot_right = [send(cot.at[lower], cot_in.at[2, lower], cot_send.at[2], cot_recv.at[2], (dp, right))]
+    for peer in along_y:
+        pl.semaphore_signal(ready_y, inc=1, device_id=(peer, me), device_id_type=MESH)
+    forward(1)
+    cot_left.append(send(cot.at[lower], cot_in.at[0, lower], cot_send.at[1], cot_recv.at[1], (dp, left)))
+    cot_right.append(send(cot.at[upper], cot_in.at[2, upper], cot_send.at[3], cot_recv.at[3], (dp, right)))
+    forward(3)
     for copy in dst_copies:
         copy.wait_recv()
-
     far_out[...] = sum_messages(2).astype(BF16)
     first_half, second_half = pl.ds(0, half_rows), pl.ds(half_rows, half_rows)
     far_right = send(far_out.at[first_half], far_in.at[0], part_send.at[0], part_recv.at[0], (dp, right))
     far_left = send(far_out.at[second_half], far_in.at[1], part_send.at[1], part_recv.at[1], (dp, left))
+    pl.semaphore_wait(ready_y, len(along_y))
+    pl.semaphore_signal(ready_core, inc=1, device_id=(other, me), device_id_type=MESH)
     partial[1] = sum_messages(1)
-    partial[2] = sum_messages(3)
-    partial[0] = sum_messages(0)
-    edge = backward(0, cot[...])
     cot_left[0].wait_recv()
     relay_left = send(cot_in.at[0, upper], cot_in.at[1, upper], cot_send.at[4], cot_recv.at[4], (dp, left))
     cot_right[0].wait_recv()
     relay_right = send(cot_in.at[2, lower], cot_in.at[1, lower], cot_send.at[5], cot_recv.at[5], (dp, right))
+    partial[2] = sum_messages(3)
+    forward(0)
     far_right.wait_recv()
     near_out[0, first_half, :] = (partial[1, first_half, :] + far_in[0].astype(F32)).astype(BF16)
     near_out[0, second_half, :] = partial[1, second_half, :].astype(BF16)
@@ -146,6 +152,9 @@
     near_out[1, first_half, :] = partial[2, first_half, :].astype(BF16)
     near_out[1, second_half, :] = (partial[2, second_half, :] + far_in[1].astype(F32)).astype(BF16)
     near_left = send(near_out.at[1], near_in.at[1], part_send.at[3], part_recv.at[3], (dp, left))
+    partial[0] = sum_messages(0)
+    edge = backward(0, cot[...])
+    pl.semaphore_wait(ready_core, 1)
 
     cot_left[1].wait_recv()
     edge = edge + backward(1, cot_in[0])
@@ -257,6 +266,7 @@
             pltpu.VMEM((shards, 3 * rows, chans), F32),
             dma((shards,)), dma((shards - 1,)), dma((shards - 1,)), dma((6,)), dma((6,)), dma((4,)), dma((4,)),
             dma((dp - 1,)), dma((dp - 1,)), dma((dp - 1,)), dma((dp - 1,)), dma((shards - 1,)), dma((shards - 1,)),
+            pltpu.SemaphoreType.REGULAR, pltpu.SemaphoreType.REGULAR,
         ],
         compiler_params=pltpu.CompilerParams(collective_id=0, has_side_effects=True, vmem_limit_bytes=VMEM_LIMIT),
         name="layer",

time: 39.8 us -> 41.6 us (1.045)
  Pallas kernels: 38.9 us -> 40.7 us
    pallas_call x1, Pallas kernels: 36.9 us -> 38.7 us  [body(): pl.pallas_call(functools.partial(layer_kernel, dp), out_shape=[shape((ato...]
where the time goes in v4:
time: 41.6 us; the launch traced here: 41.3 us
  Pallas kernels  40.7 us (98%)
  between operations  0.64 us (2%)
    pallas_call x1, Pallas kernels, body(): pl.pallas_call(functools.partial(layer_kernel, dp), out_shape=[shape((ato...  38.7 us
    pallas_call x1, Pallas kernels, body(): pl.pallas_call(results_kernel, out_shape=[shape((atom_count, chans), BF16...  2.01 us

profile of v4, /device:TPU:0, one launch (start us, length us, event | category | flops | bytes accessed | tf_op | source)
XLA Modules:
  0.0 41.3 jit_solution(10657571612941649576)
XLA Ops:
  0.6 38.7 %layer.1 = (bf16[1024,128]{1,0:T(8,128)(2,1)}, bf16[1024,128]{1,0:T(8,128)(2,1)}, f32[12,128]{1,0:T(8,128)}) custom-call(s32[4,4]{1,0:T(4,128)} %bitcast.15, bf16[1024,128]{1,0:T(8,128)(2,1)} %bitcast.11, f32[1,128]{1,0:T(1,128)} %bitcast.16, bf16[128,128]{1,0:T(8,128)(2,1)} %w_src.3, bf16[128,128]{1,0:T(8,128)(2,1)} %w_edge.1, bf16[128,128]{1,0:T(8,128)(2,1)} %w_out.1, ...), custom_call_target="tpu_custom_call" | custom-call | tf_op jit(solution)/shard_map/layer/pallas_call | solution.py:244
  39.3 2.0 %results.1 = (bf16[1024,128]{1,0:T(8,128)(2,1)}, bf16[1024,128]{1,0:T(8,128)(2,1)}, f32[4,128]{1,0:T(4,128)}, f32[4,128]{1,0:T(4,128)}, f32[4,128]{1,0:T(4,128)}, /*index=5*/f32[1,4]{1,0:T(1,128)}) custom-call(f32[1,128]{1,0:T(1,128)} %bitcast.17, bf16[128,128]{1,0:T(8,128)(2,1)} %w_src.3, bf16[1024,128]{1,0:T(8,128)(2,1)} %get-tuple-element.15.layer, ...), custom_call_target="tpu_custom_call" | custom-call | tf_op jit(solution)/shard_map/results/pallas_call | solution.py:278
